TPU v7x, 512 devices: a whole 4x8x8 slice. The times are simulated.
512 devices in a mesh: seq: 64 (over z, x, y_hi), ch: 8 (over y_lo, core).
Axes of the slice: x: 4, y: 8 (y_hi: 2, y_lo: 4; y = y_hi * 4 + y_lo), z: 8, core: 2. Of those that a mesh axis runs over, the one named last changes fastest.
Arguments:
- queries: bfloat16 [4096, 8192], P('ch', 'seq'), may hold values from -6 to 6
- key_feat: bfloat16 [4096, 8192], P('ch', 'seq'), may hold values from -6 to 6
- value_feat: bfloat16 [4096, 8192], P('ch', 'seq'), may hold values from -6 to 6
- out_grad: bfloat16 [4096, 8192], P('ch', 'seq'), may hold values from -6 to 6
- out_weight: bfloat16 [4096, 4096], P('ch', 'seq'), may hold values from -0.09375 to 0.09375
- long_filter: bfloat16 [4096, 8192], P('ch', 'seq'), may hold values from -0.125 to 0.125
- short_filter: bfloat16 [256, 128], P('ch'), may hold values from -0.5 to 0.5
Outputs:
- d_key: bfloat16 [4096, 8192], P('ch', 'seq')
- d_value: bfloat16 [4096, 8192], P('ch', 'seq')
- d_filter: float32 [256, 128], P('ch')
All inputs are finite; a program needn't handle non-finite values.
Results may differ from a plain program's by a relative error of at most 0.0064.
Values may be sent and summed in bfloat16 or wider, within the bound.
No kernel may reach another device: no remote copies, remote signals or barrier semaphores. Data moves between devices by JAX's collectives and lax.ppermute only.
A program may use at most 64 MiB of HBM per device.

v0:
```python
import math

import jax
import jax.numpy as jnp
from jax import lax
from jax.sharding import PartitionSpec as P

highest = lax.Precision.HIGHEST


def from_behind(value, axis, steps):
    count = lax.axis_size(axis)
    first, last = (max(0, -steps), min(count, count - steps))
    return lax.ppermute(value, axis, [(source, source + steps) for source in range(first, last)])


def angle_table(first, second, modulus):
    left = lax.broadcasted_iota(jnp.int32, (first, second), 0)
    right = lax.broadcasted_iota(jnp.int32, (first, second), 1)
    phase = (left * right % modulus).astype(jnp.float32) * (2.0 * math.pi / modulus)
    return (jnp.cos(phase), jnp.sin(phase))


def contract(form, first, second):
    return jnp.einsum(form, first, second, precision=highest)


def spectral(pair):
    grads, filters = pair
    items = grads.shape[1]
    seq_len = grads.shape[2]
    inner = 128
    half = seq_len // inner
    outer = 2 * half
    total_len = outer * inner
    cos_p, sin_p = angle_table(outer, half, outer)
    cos_t, sin_t = angle_table(outer, inner, total_len)
    cos_q, sin_q = angle_table(inner, inner, inner)

    def forward(signal):
        series = signal.astype(jnp.float32).reshape(items, half, inner)
        first_re = contract("kn,cnq->ckq", cos_p, series)
        first_im = -contract("kn,cnq->ckq", sin_p, series)
        turned_re = first_re * cos_t + first_im * sin_t
        turned_im = first_im * cos_t - first_re * sin_t
        spec_re = contract("ckq,qm->ckm", turned_re, cos_q) + contract(
            "ckq,qm->ckm", turned_im, sin_q
        )
        spec_im = contract("ckq,qm->ckm", turned_im, cos_q) - contract(
            "ckq,qm->ckm", turned_re, sin_q
        )
        return (spec_re, spec_im)

    grad_re, grad_im = forward(grads[0])
    filt_re, filt_im = forward(filters[0])
    prod_re = filt_re * grad_re + filt_im * grad_im
    prod_im = filt_re * grad_im - filt_im * grad_re
    back_re = contract("ckq,qm->ckm", prod_re, cos_q) - contract("ckq,qm->ckm", prod_im, sin_q)
    back_im = contract("ckq,qm->ckm", prod_im, cos_q) + contract("ckq,qm->ckm", prod_re, sin_q)
    twist_re = back_re * cos_t - back_im * sin_t
    twist_im = back_im * cos_t + back_re * sin_t
    result = contract("kn,ckq->cnq", cos_p, twist_re) - contract("kn,ckq->cnq", sin_p, twist_im)
    return (result / total_len).reshape(1, items, seq_len).astype(jnp.bfloat16)


def windows(extended, group_count, per_group, block_count, tap_count):
    parts = extended.reshape(group_count, per_group, block_count + 1, tap_count)
    return jnp.concatenate([parts[:, :, :-1], parts[:, :, 1:]], axis=3)


def local(queries, key_feat, value_feat, out_grad, out_weight, long_filter, short_filter):
    seq_devices = lax.axis_size("seq")
    channels, row_count = out_grad.shape
    group_count, tap_count = short_filter.shape
    per_group = channels // group_count
    block_count = row_count // tap_count
    per_device = channels // seq_devices
    whole = lax.all_gather(out_grad, "ch", axis=0, tiled=True)
    d_z = jnp.dot(
        lax.all_gather(out_weight, "seq", axis=1, tiled=True),
        whole,
        preferred_element_type=jnp.float32,
    )
    d_c = (d_z * queries.astype(jnp.float32)).astype(jnp.bfloat16)
    packed = (
        d_c.reshape(seq_devices, per_device, row_count),
        long_filter.reshape(seq_devices, per_device, row_count),
    )
    d_w = spectral(
        (
            lax.all_to_all(packed[0], "seq", split_axis=0, concat_axis=2, tiled=True),
            lax.all_to_all(packed[1], "seq", split_axis=0, concat_axis=2, tiled=True),
        )
    )
    prev_rows = from_behind(value_feat, "seq", 1)
    ext_values = jnp.concatenate([prev_rows, value_feat], axis=1)
    value_win = windows(ext_values, group_count, per_group, block_count, tap_count)
    padded_filter = jnp.pad(short_filter, ((0, 0), (0, tap_count + 1)))
    toeplitz = jnp.tile(padded_filter, (1, tap_count))[:, : 2 * tap_count * tap_count]
    toeplitz = toeplitz.reshape(group_count, tap_count, 2 * tap_count)
    reversed_out = jnp.einsum(
        "gtw,gcbw->gcbt", toeplitz, value_win[..., ::-1], preferred_element_type=jnp.float32
    )
    filtered = reversed_out[..., ::-1].reshape(channels, row_count)
    back = lax.all_to_all(d_w, "seq", split_axis=2, concat_axis=0, tiled=True)
    d_w_local = back.reshape(channels, row_count)
    d_vf = (d_w_local.astype(jnp.float32) * key_feat.astype(jnp.float32)).astype(jnp.bfloat16)
    ahead = from_behind(d_vf, "seq", -1)
    ext_grads = jnp.concatenate([d_vf, ahead], axis=1)
    d_key = (d_w_local.astype(jnp.float32) * filtered).astype(jnp.bfloat16)
    grad_win = windows(ext_grads, group_count, per_group, block_count, tap_count)
    d_value = jnp.einsum("gtw,gcbw->gcbt", toeplitz, grad_win, preferred_element_type=jnp.float32)
    d_value = d_value.reshape(channels, row_count).astype(jnp.bfloat16)
    grads_blocked = d_vf.reshape(group_count, per_group, block_count, tap_count)
    corr = jnp.einsum(
        "gcbt,gcbw->gtw", grads_blocked, value_win, preferred_element_type=jnp.float32
    )
    flat = corr.reshape(group_count, 2 * tap_count * tap_count)
    flat = jnp.pad(flat, ((0, 0), (0, tap_count)))
    skewed = flat.reshape(group_count, tap_count, 2 * tap_count + 1)
    column_sums = jnp.sum(skewed, axis=1)
    local_part = column_sums[:, 1 : tap_count + 1][:, ::-1]
    summed = lax.psum(local_part, "seq")
    scale_factor = 1.0 / math.sqrt(row_count * seq_devices * per_group)
    return (d_key, d_value, summed * scale_factor)


def solution(mesh):
    placed = (
        P("ch", "seq"),
        P("ch", "seq"),
        P("ch", "seq"),
        P("ch", "seq"),
        P("ch", "seq"),
        P("ch", "seq"),
        P("ch", None),
    )
    return jax.shard_map(
        local,
        mesh=mesh,
        in_specs=placed,
        out_specs=(P("ch", "seq"), P("ch", "seq"), P("ch", None)),
        check_vma=False,
    )
```

profile of v0, /device:TPU:16, one launch (start us, length us, event | category | flops | bytes accessed | tf_op | source)
XLA Modules:
  0.0 815.4 jit_solution(5035333514818780619)
XLA Ops:
  8.6 5.9 collective-permute-start
  14.6 15.8 %all-to-all-start = ((bf16[64,8,128]{2,1,0:T(8,128)(2,1)}), bf16[64,8,128]{2,1,0:T(8,128)(2,1)S(1)}, u32[]{:S(2)}, u32[]{:S(2)}) async-start(bf16[64,8,128]{2,1,0:T(8,128)(2,1)} %bitcast.129), calls=%async_computation | async-start | bytes 262144 | tf_op jit(solution)/shard_map/all_to_all | solution.py:92
  31.6 2.0 tile.4
  33.5 6.2 tile.10
  39.7 1.6 slice-done
  43.4 3.3 all-to-all-done
  48.6 1.6 convolution_add_fusion.2
  50.2 161.0 %all-gather.3.cloned.1.call-done = bf16[512,4096]{0,1:T(8,128)(2,1)} async-done(((bf16[512,64]{0,1:T(8,128)(2,1)}), bf16[512,4096]{0,1:T(8,128)(2,1)}) %all-gather.3.cloned.1.call-update) | async-done | bytes 4194320 | tf_op jit(solution)/shard_map/all_gather | solution.py:80
  211.2 4.5 fusion.5
  215.7 9.9 %all-to-all-start.1 = ((bf16[64,8,128]{2,1,0:T(8,128)(2,1)}), bf16[64,8,128]{2,1,0:T(8,128)(2,1)S(1)}, u32[]{:S(2)}, u32[]{:S(2)}) async-start(bf16[64,8,128]{2,1,0:T(8,128)(2,1)} %fusion.5), calls=%async_computation.1 | async-start | bytes 262144 | tf_op jit(solution)/shard_map/all_to_all | solution.py:91
  225.7 1.6 fusion.6
  227.3 13.1 %all-to-all-done.1 = bf16[64,8,128]{2,1,0:T(8,128)(2,1)S(1)} async-done(((bf16[64,8,128]{2,1,0:T(8,128)(2,1)}), bf16[64,8,128]{2,1,0:T(8,128)(2,1)S(1)}, u32[]{:S(2)}, u32[]{:S(2)}) %all-to-all-start.1) | async-done | bytes 131104 | tf_op jit(solution)/shard_map/all_to_all | solution.py:91
  241.5 1.2 fusion.41
  242.7 1.2 fusion.40
  243.9 1.2 convolution_subtract_fusion.1
  245.1 1.2 convolution_add_fusion.1
  251.6 1.1 fusion.4
  252.8 6.7 copy.55
  260.0 46.6 %reduce = bf16[8192,8]{1,0:T(8,128)(2,1)} reduce(bf16[8192,1,8]{2,1,0:T(2,128)(2,1)} %bitcast.122, bf16[]{:T(256)} %broadcast.142), dimensions={1}, to_apply=%bitcast.104.reduce_sub_computation | reduce | bytes 262146
  306.6 4.3 reshape.131
  310.9 4.6 all-to-all-start.2
  316.3 13.9 %all-to-all-done.2 = bf16[64,2,512]{2,1,0:T(2,128)(2,1)S(1)} async-done(((bf16[64,2,512]{2,1,0:T(2,128)(2,1)}), bf16[64,2,512]{2,1,0:T(2,128)(2,1)S(1)}, u32[]{:S(2)}, u32[]{:S(2)}) %all-to-all-start.2) | async-done | bytes 131104 | tf_op jit(solution)/shard_map/all_to_all | solution.py:105
  330.2 8.7 %reshape.132 = bf16[8192,1,8]{2,1,0:T(2,128)(2,1)} reshape(bf16[64,2,512]{2,1,0:T(2,128)(2,1)S(1)} %all-to-all-done.2) | data formatting | bytes 262144
  338.9 8.5 %bitcast_convert_fusion = f32[1,8,8192]{1,0,2:T(1,128)} fusion(bf16[8192,1,8]{2,1,0:T(2,128)(2,1)} %reshape.132), kind=kLoop, calls=%fused_computation.195 | loop fusion | flops 65536 | bytes 393216 | tf_op jit(solution)/shard_map/convert_element_type | solution.py:110
  347.4 2.8 copy.56
  350.9 1.5 collective-permute-start.1
  353.2 2.4 copy.76
  355.6 2.3 pad.9
  357.9 8.0 reshape.124
  365.9 3.3 reduce_sum.9
  369.4 436.5 %psum.7 = f32[32,128]{1,0:T(8,128)S(1)} all-reduce(f32[32,128]{1,0:T(8,128)S(1)} %rev.8), channel_id=1, replica_groups=mesh['seq'=64,'ch'=8] {'seq'}, use_global_device_ids=true, to_apply=%region_1.2 | all-reduce | flops 4096 | bytes 32768 | tf_op jit(solution)/shard_map/psum | solution.py:123
  807.0 1.3 convolution_convert_fusion
  (58 shorter events, 16.8 us)
Async XLA Ops:
  7.2 43.0 %all-gather.5.cloned.1.call-start = ((), (), s32[]{:S(2)}) async-start(), calls=%async_computation.4 | async-start | bytes 1179648 | tf_op jit(solution)/shard_map/all_gather | solution.py:78
  7.9 203.3 %all-gather.3.cloned.1.call-start = ((), (), s32[]{:S(2)}) async-start(), calls=%async_computation.3 | async-start | bytes 4259840 | tf_op jit(solution)/shard_map/all_gather | solution.py:80
  8.6 33.2 %collective-permute-start = (bf16[512,128]{1,0:T(8,128)(2,1)}, bf16[512,128]{1,0:T(8,128)(2,1)S(1)}, u32[]{:S(2)}, u32[]{:S(2)}) collective-permute-start(bf16[512,128]{1,0:T(8,128)(2,1)} %param.9), channel_id=1, source_target_pairs={{0,8},{8,16},{16,24},{24,32},{32,40},{40,48},{48,56},{56,64},{64,7... | collective-permute-start | bytes 393224 | tf_op jit(solution)/shard_map/ppermute | solution.py:14
  14.6 32.1 %all-to-all-start = ((bf16[64,8,128]{2,1,0:T(8,128)(2,1)}), bf16[64,8,128]{2,1,0:T(8,128)(2,1)S(1)}, u32[]{:S(2)}, u32[]{:S(2)}) async-start(bf16[64,8,128]{2,1,0:T(8,128)(2,1)} %bitcast.129), calls=%async_computation | async-start | bytes 262144 | tf_op jit(solution)/shard_map/all_to_all | solution.py:92
  39.7 1.6 slice-start
  39.7 2.1 copy-start.6
  42.4 1.0 copy-start.2
  215.7 24.7 %all-to-all-start.1 = ((bf16[64,8,128]{2,1,0:T(8,128)(2,1)}), bf16[64,8,128]{2,1,0:T(8,128)(2,1)S(1)}, u32[]{:S(2)}, u32[]{:S(2)}) async-start(bf16[64,8,128]{2,1,0:T(8,128)(2,1)} %fusion.5), calls=%async_computation.1 | async-start | bytes 262144 | tf_op jit(solution)/shard_map/all_to_all | solution.py:91
  240.9 5.4 copy-start
  240.9 5.4 copy-start.1
  260.0 55.6 %copy-start.4 = (bf16[32,16,1,256]{3,1,0,2:T(8,128)(2,1)S(1)}, bf16[32,16,1,256]{3,1,0,2:T(8,128)(2,1)}, u32[]{:S(2)}) copy-start(bf16[32,16,1,256]{3,1,0,2:T(8,128)(2,1)} %rev.7) | copy-start | bytes 786436
  310.9 19.3 %all-to-all-start.2 = ((bf16[64,2,512]{2,1,0:T(2,128)(2,1)}), bf16[64,2,512]{2,1,0:T(2,128)(2,1)S(1)}, u32[]{:S(2)}, u32[]{:S(2)}) async-start(bf16[64,2,512]{2,1,0:T(2,128)(2,1)} %reshape.131), calls=%async_computation.2 | async-start | bytes 262144 | tf_op jit(solution)/shard_map/all_to_all | solution.py:105
  347.4 2.8 copy-start.5
  347.4 5.1 copy-start.3
  350.9 455.6 %collective-permute-start.1 = (bf16[512,128]{1,0:T(8,128)(2,1)S(1)}, bf16[512,128]{1,0:T(8,128)(2,1)S(1)}, u32[]{:S(2)}, u32[]{:S(2)}) collective-permute-start(bf16[512,128]{1,0:T(8,128)(2,1)S(1)} %get-tuple-element.7), channel_id=1, source_target_pairs={{8,0},{16,8},{24,16},{32,24},{40,32},{48,40},{56,48},{64,56},{72,6... | collective-permute-start | bytes 393224 | tf_op jit(solution)/shard_map/ppermute | solution.py:14
Sparse Core Ops, SparseCore 0:
  10.0 38.5 all-gather.4
  53.0 158.1 all-gather.2
where the time goes:
time: 823 us; the launch traced here: 815 us
  blocking collectives  436 us (53%)
  waiting for transfers between devices  193 us (23%)
  other arithmetic  60 us (7%)
  local copies, waits for them, and re-layouts  49.3 us (6%)
  starting transfers between devices  37.8 us (5%)
  matrix products  24.5 us (3%)
  between operations  14.6 us (2%)
    psum x1, blocking collectives, local(): summed = lax.psum(local_part, 'seq')  436 us
    all_gather x1, waiting for transfers between devices, local(): lax.all_gather(out_weight, 'seq', axis=1, tiled=True)  161 us
    unnamed x1, other arithmetic  46.6 us
    dot_general x18, matrix products, contract(): return jnp.einsum(form, first, second, precision=highest)  17.3 us
    unnamed x22, local copies, waits for them, and re-layouts  16.5 us
  transfers between devices with their start and end apart: 7, of which 4 were waited for; matrix products, arithmetic and copies ran while one was open for 4% of the time, Pallas kernels for 0%

commit v1 on v0

v1 whole, which is shorter than its diff:
```python
import math

import jax
import jax.numpy as jnp
from jax import lax
from jax.sharding import Mesh, PartitionSpec as P

highest = lax.Precision.HIGHEST
SEQ = ("z", "x", "yh")
CH = ("yl", "core")
SPLIT = {"z": 8, "x": 4, "yh": 2, "yl": 4, "core": 2}


def swap(value, axes):
    return lax.all_to_all(value, axes, split_axis=0, concat_axis=0, tiled=True)


def angle_table(first, second, modulus):
    left = lax.broadcasted_iota(jnp.int32, (first, second), 0)
    right = lax.broadcasted_iota(jnp.int32, (first, second), 1)
    phase = (left * right % modulus).astype(jnp.float32) * (2.0 * math.pi / modulus)
    return (jnp.cos(phase), jnp.sin(phase))


def contract(form, first, second):
    return jnp.einsum(form, first, second, precision=highest)


def spectral(grads, filters):
    half, items, inner = grads.shape
    outer = 2 * half
    total_len = outer * inner
    cos_p, sin_p = angle_table(outer, half, outer)
    cos_t, sin_t = angle_table(outer, inner, total_len)
    cos_q, sin_q = angle_table(inner, inner, inner)

    def forward(series):
        series = series.astype(jnp.float32)
        first_re = contract("kn,ncq->ckq", cos_p, series)
        first_im = -contract("kn,ncq->ckq", sin_p, series)
        turned_re = first_re * cos_t + first_im * sin_t
        turned_im = first_im * cos_t - first_re * sin_t
        spec_re = contract("ckq,qm->ckm", turned_re, cos_q) + contract(
            "ckq,qm->ckm", turned_im, sin_q
        )
        spec_im = contract("ckq,qm->ckm", turned_im, cos_q) - contract(
            "ckq,qm->ckm", turned_re, sin_q
        )
        return (spec_re, spec_im)

    grad_re, grad_im = forward(grads)
    filt_re, filt_im = forward(filters)
    prod_re = filt_re * grad_re + filt_im * grad_im
    prod_im = filt_re * grad_im - filt_im * grad_re
    back_re = contract("ckq,qm->ckm", prod_re, cos_q) - contract("ckq,qm->ckm", prod_im, sin_q)
    back_im = contract("ckq,qm->ckm", prod_im, cos_q) + contract("ckq,qm->ckm", prod_re, sin_q)
    twist_re = back_re * cos_t - back_im * sin_t
    twist_im = back_im * cos_t + back_re * sin_t
    result = contract("kn,ckq->ncq", cos_p, twist_re) - contract("kn,ckq->ncq", sin_p, twist_im)
    return result / total_len


def local(queries, key_feat, value_feat, out_grad, out_weight, long_filter, short_filter):
    channels, row_count = out_grad.shape
    group_count, tap_count = short_filter.shape
    per_group = channels // group_count
    split = SPLIT["x"] * SPLIT["yh"]
    seq_devices = SPLIT["z"] * split
    items = channels // seq_devices
    features = out_weight.shape[1]

    pieces = [
        a.reshape(seq_devices, items, row_count)
        for a in (long_filter, key_feat, value_feat, queries)
    ]
    moved = swap(jnp.concatenate(pieces, axis=1), SEQ)
    filters, keys, values, gates = jnp.split(moved, 4, axis=1)

    weight = jnp.broadcast_to(out_weight.T[None], (SPLIT["z"], features, channels))
    weight = swap(weight, ("z",))
    weight = weight.reshape(SPLIT["yl"], SPLIT["core"], features, channels)
    grad = out_grad.reshape(split, 1, features, row_count)
    grad = jnp.broadcast_to(grad, (split, SPLIT["yl"], features, row_count))
    grad = swap(grad.reshape(split * SPLIT["yl"], features, row_count), ("x", "yh", "yl"))
    grad = jnp.broadcast_to(grad[None], (SPLIT["core"],) + grad.shape)
    grad = swap(grad, ("core",))
    grad = grad.reshape(SPLIT["core"], split, SPLIT["yl"], features, row_count)
    partial = jnp.einsum(
        "ycoi,csyot->sit", weight, grad, preferred_element_type=jnp.float32
    ).astype(jnp.bfloat16)
    partial = partial.reshape(split, seq_devices, items, row_count).transpose(1, 0, 2, 3)
    partial = swap(partial, SEQ)
    partial = partial.reshape(SPLIT["z"], split, split, items, row_count)
    d_z = jnp.sum(partial.astype(jnp.float32), axis=1).reshape(seq_devices, items, row_count)
    d_c = (d_z * gates.astype(jnp.float32)).astype(jnp.bfloat16)

    d_w = spectral(d_c, filters).astype(jnp.bfloat16).astype(jnp.float32)
    place = lax.axis_index(SEQ) * items // per_group
    taps = lax.dynamic_slice_in_dim(short_filter, place, 1, 0)
    lag = lax.broadcasted_iota(jnp.int32, (tap_count, 2 * tap_count), 1) - lax.broadcasted_iota(
        jnp.int32, (tap_count, 2 * tap_count), 0
    )
    padded = jnp.pad(taps[0], (0, tap_count + 1))
    toeplitz = jnp.tile(padded, tap_count)[: 2 * tap_count * tap_count]
    toeplitz = toeplitz.reshape(tap_count, 2 * tap_count)
    zero = jnp.zeros((1, items, row_count), jnp.bfloat16)
    value_win = jnp.concatenate(
        [jnp.concatenate([zero, values[:-1]], axis=0), values], axis=2
    )
    filtered = jnp.einsum(
        "tw,bcw->bct", toeplitz[::-1, ::-1], value_win, preferred_element_type=jnp.float32
    )
    d_key = (d_w * filtered).astype(jnp.bfloat16)
    d_vf = (d_w * keys.astype(jnp.float32)).astype(jnp.bfloat16)
    grad_win = jnp.concatenate(
        [d_vf, jnp.concatenate([d_vf[1:], zero], axis=0)], axis=2
    )
    d_value = jnp.einsum(
        "tw,bcw->bct", toeplitz, grad_win, preferred_element_type=jnp.float32
    ).astype(jnp.bfloat16)
    corr = jnp.einsum("bct,bcw->tw", d_vf, value_win, preferred_element_type=jnp.float32)
    flat = jnp.pad(corr.reshape(-1), (0, tap_count))
    skewed = flat.reshape(tap_count, 2 * tap_count + 1)
    part = jnp.sum(skewed, axis=0)[1 : tap_count + 1][::-1]
    scale_factor = 1.0 / math.sqrt(row_count * seq_devices * per_group)
    part = part * scale_factor
    high = part.astype(jnp.bfloat16)
    low = (part - high.astype(jnp.float32)).astype(jnp.bfloat16)
    both = jnp.concatenate([high[None], low[None], jnp.zeros((items - 2, tap_count), jnp.bfloat16)])
    both = jnp.broadcast_to(both[None], (seq_devices, items, tap_count))
    home = swap(jnp.concatenate([d_key, d_value, both], axis=1), SEQ)
    d_key, d_value, both = jnp.split(home, 3, axis=1)
    both = both[:, 0].astype(jnp.float32) + both[:, 1].astype(jnp.float32)
    d_filter = jnp.sum(both.reshape(group_count, seq_devices // group_count, tap_count), axis=1)
    return (d_key.reshape(channels, row_count), d_value.reshape(channels, row_count), d_filter)


def solution(mesh):
    fine = Mesh(mesh.devices.reshape(tuple(SPLIT.values())), tuple(SPLIT))
    placed = (P(CH, SEQ),) * 6 + (P(CH, None),)
    return jax.shard_map(
        local,
        mesh=fine,
        in_specs=placed,
        out_specs=(P(CH, SEQ), P(CH, SEQ), P(CH, None)),
        check_vma=False,
    )
```

time: 823 us -> 169 us (0.21)
  blocking collectives: 436 us -> 55.8 us
  waiting for transfers between devices: 193 us -> 59.8 us
  other arithmetic: 60 us -> 2.49 us
  local copies, waits for them, and re-layouts: 49.3 us -> 8.62 us
  starting transfers between devices: 37.8 us -> 21.6 us
  between operations: 14.6 us -> 1.1 us
    psum x1 -> x0, blocking collectives: 436 us -> none  [local(): summed = lax.psum(local_part, 'seq')]
    all_gather x2 -> x0, waiting for transfers between devices: 161 us -> none  [the longest x1 161 us: local(): lax.all_gather(out_weight, 'seq', axis=1, tiled=True)]
    all_to_all x0 -> x3, blocking collectives: none -> 55.8 us  [swap(): return lax.all_to_all(value, axes, split_axis=0, concat_axis=0, tiled=True)]
    unnamed x1 -> x0, other arithmetic: 46.6 us -> none
    all_to_all x3, waiting for transfers between devices: 30.3 us -> 59.8 us  [swap(): return lax.all_to_all(value, axes, split_axis=0, concat_axis=0, tiled=True)]
    unnamed x22 -> x21, local copies, waits for them, and re-layouts: 16.5 us -> 0.16 us
    convert_element_type x2 -> x1, other arithmetic: 9.17 us -> 0.03 us  [local(): d_c = (d_z * gates.astype(jnp.float32)).astype(jnp.bfloat16)]
    convert_element_type x3 -> x1, local copies, waits for them, and re-layouts: 9.6 us -> 0.66 us  [local(): partial = jnp.einsum('ycoi,csyot->sit', weight, grad, preferred_element_t...]
  transfers between devices with their start and end apart: 7 -> 3, of which waited for: 4 -> 3; matrix products, arithmetic and copies ran while one was open for 4% -> 7% of each run, Pallas kernels for 0% -> 0%
where the time goes in v1:
time: 169 us
  waiting for transfers between devices  59.8 us (35%)
  blocking collectives  55.8 us (33%)
  starting transfers between devices  21.6 us (13%)
  matrix products  19.3 us (11%)
  local copies, waits for them, and re-layouts  8.62 us (5%)
  other arithmetic  2.49 us (1%)
    all_to_all x3, waiting for transfers between devices, swap(): return lax.all_to_all(value, axes, split_axis=0, concat_axis=0, tiled=True)  59.8 us
    all_to_all x3, blocking collectives, swap(): return lax.all_to_all(value, axes, split_axis=0, concat_axis=0, tiled=True)  55.8 us
    all_to_all x3, starting transfers between devices, swap(): return lax.all_to_all(value, axes, split_axis=0, concat_axis=0, tiled=True)  21.6 us
    dot_general x18, matrix products, contract(): return jnp.einsum(form, first, second, precision=highest)  17.9 us
  transfers between devices with their start and end apart: 3, of which 3 were waited for; matrix products, arithmetic and copies ran while one was open for 7% of the time, Pallas kernels for 0%

profile of v1, /device:TPU:16, one launch (start us, length us, event | category | flops | bytes accessed | tf_op | source)
XLA Modules:
  0.0 168.7 jit_solution(13075267445127823980)
XLA Ops:
  0.7 0.9 broadcast_in_dim.19
  1.6 27.6 %all_to_all.30 = bf16[8,64,512]{2,1,0:T(8,128)(2,1)S(1)} all-to-all(bf16[8,64,512]{2,1,0:T(8,128)(2,1)S(1)} %broadcast_in_dim.19), channel_id=1, replica_groups=mesh['z'=8,'x'=4,'yh'=2,'yl'=4,'core'=2] {'z'}, dimensions={0} | all-to-all | bytes 1048576 | tf_op jit(solution)/shard_map/all_to_all | solution.py:15
  29.2 0.9 broadcast_in_dim.17
  30.1 10.0 %all-to-all-start.1 = ((bf16[32,64,128]{2,1,0:T(8,128)(2,1)}), bf16[32,64,128]{2,1,0:T(8,128)(2,1)S(1)}, u32[]{:S(2)}, u32[]{:S(2)}) async-start(bf16[32,64,128]{2,1,0:T(8,128)(2,1)} %bitcast.11), calls=%async_computation.1 | async-start | bytes 1048576 | tf_op jit(solution)/shard_map/all_to_all | solution.py:15
  40.2 0.9 pad_maximum_fusion
  41.1 13.9 %all-to-all-done.1 = bf16[32,64,128]{2,1,0:T(8,128)(2,1)S(1)} async-done(((bf16[32,64,128]{2,1,0:T(8,128)(2,1)}), bf16[32,64,128]{2,1,0:T(8,128)(2,1)S(1)}, u32[]{:S(2)}, u32[]{:S(2)}) %all-to-all-start.1) | async-done | bytes 524320 | tf_op jit(solution)/shard_map/all_to_all | solution.py:15
  55.3 4.6 %all_to_all.31 = bf16[2,32,64,128]{3,2,1,0:T(8,128)(2,1)S(1)} all-to-all(bf16[2,32,64,128]{3,2,1,0:T(8,128)(2,1)S(1)} %broadcast_in_dim.18), channel_id=1, replica_groups=mesh['z'=8,'x'=4,'yh'=2,'yl'=4,'core'=2] {'core'}, dimensions={0} | all-to-all | bytes 2097152 | tf_op jit(solution)/shard_map/all_to_all | solution.py:15
  59.9 6.8 %all-to-all-start = ((bf16[64,32,128]{2,1,0:T(8,128)(2,1)}), bf16[64,32,128]{2,1,0:T(8,128)(2,1)S(1)}, u32[]{:S(2)}, u32[]{:S(2)}) async-start(bf16[64,32,128]{2,1,0:T(8,128)(2,1)} %pad_maximum_fusion), calls=%async_computation | async-start | bytes 1048576 | tf_op jit(solution)/shard_map/all_to_all | solution.py:15
  66.6 0.7 fusion
  67.4 0.7 copy.94
  68.0 1.3 copy.95
  69.3 20.8 %all-to-all-done = bf16[64,32,128]{2,1,0:T(8,128)(2,1)S(1)} async-done(((bf16[64,32,128]{2,1,0:T(8,128)(2,1)}), bf16[64,32,128]{2,1,0:T(8,128)(2,1)S(1)}, u32[]{:S(2)}, u32[]{:S(2)}) %all-to-all-start) | async-done | bytes 524320 | tf_op jit(solution)/shard_map/all_to_all | solution.py:15
  90.1 4.8 %all-to-all-start.4 = ((bf16[64,8,8,128]{3,2,1,0:T(8,128)(2,1)}), bf16[64,8,8,128]{3,2,1,0:T(8,128)(2,1)S(1)}, u32[]{:S(2)}, u32[]{:S(2)}) async-start(bf16[64,8,8,128]{3,2,1,0:T(8,128)(2,1)} %copy.95), calls=%async_computation.4 | async-start | bytes 2097152 | tf_op jit(solution)/shard_map/all_to_all | solution.py:15
  96.8 0.8 rev.6
  97.7 0.7 fusion.177
  99.5 1.2 fusion.35
  100.7 2.0 %fusion.36 = f32[8,128,128]{2,1,0:T(8,128)} fusion(f32[8,128,128]{1,2,0:T(8,128)S(1)} %convolution_bitcast_fusion.1, f32[8,128,128]{1,2,0:T(8,128)S(1)} %fusion.2, f32[128,128]{0,1:T(8,128)S(1)} %copy.90, f32[128,128]{0,1:T(8,128)S(1)} %copy.89), kind=kOutput, calls=%fused_computation.65 | convolution fusion | flops 201949184 | bytes 1703936 | tf_op jit(solution)/shard_map/ckq,qm->ckm/dot_general | solution.py:26
  102.7 1.2 convolution_add_fusion.2
  103.9 25.1 %all-to-all-done.4 = bf16[64,8,8,128]{3,2,1,0:T(8,128)(2,1)S(1)} async-done(((bf16[64,8,8,128]{3,2,1,0:T(8,128)(2,1)}), bf16[64,8,8,128]{3,2,1,0:T(8,128)(2,1)S(1)}, u32[]{:S(2)}, u32[]{:S(2)}) %all-to-all-start.4) | async-done | bytes 1048608 | tf_op jit(solution)/shard_map/all_to_all | solution.py:15
  130.3 1.2 fusion.38
  131.5 1.2 fusion.37
  132.7 1.2 convolution_subtract_fusion.1
  133.9 1.2 convolution_add_fusion.1
  135.1 1.5 multiply_add_fusion
  136.6 0.9 fusion.50
  137.5 0.9 fusion.52
  138.4 0.9 convolution_add_fusion
  139.2 0.9 convolution_subtract_fusion
  140.1 0.8 fusion.11
  141.0 0.8 multiply_convert_fusion
  143.7 23.6 %all_to_all.32 = bf16[64,24,128]{2,1,0:T(8,128)(2,1)S(1)} all-to-all(bf16[64,24,128]{2,1,0:T(8,128)(2,1)S(1)} %copy.117), channel_id=1, replica_groups=mesh['z'=8,'x'=4,'yh'=2,'yl'=4,'core'=2] {'z','x','yh'}, dimensions={0} | all-to-all | bytes 786432 | tf_op jit(solution)/shard_map/all_to_all | solution.py:15
  168.0 0.7 slice_bitcast_fusion
  (59 shorter events, 6.9 us)
Async XLA Ops:
  0.6 94.3 %copy-start = (bf16[32,128]{1,0:T(8,128)(2,1)S(1)}, bf16[32,128]{1,0:T(8,128)(2,1)}, u32[]{:S(2)}) copy-start(bf16[32,128]{1,0:T(8,128)(2,1)} %param.13) | copy-start | bytes 24580
  0.6 28.6 %copy-start.4 = (bf16[512,128]{1,0:T(8,128)(2,1)S(1)}, bf16[512,128]{1,0:T(8,128)(2,1)}, u32[]{:S(2)}) copy-start(bf16[512,128]{1,0:T(8,128)(2,1)} %param.10) | copy-start | bytes 393220
  29.2 11.0 %copy-start.5 = (bf16[512,128]{1,0:T(8,128)(2,1)S(1)}, bf16[512,128]{1,0:T(8,128)(2,1)}, u32[]{:S(2)}) copy-start(bf16[512,128]{1,0:T(8,128)(2,1)} %param.7) | copy-start | bytes 393220
  29.2 11.0 %copy-start.6 = (bf16[512,128]{1,0:T(8,128)(2,1)S(1)}, bf16[512,128]{1,0:T(8,128)(2,1)}, u32[]{:S(2)}) copy-start(bf16[512,128]{1,0:T(8,128)(2,1)} %param.9) | copy-start | bytes 393220
  29.2 11.0 %copy-start.7 = (bf16[512,128]{1,0:T(8,128)(2,1)S(1)}, bf16[512,128]{1,0:T(8,128)(2,1)}, u32[]{:S(2)}) copy-start(bf16[512,128]{1,0:T(8,128)(2,1)} %param.8) | copy-start | bytes 393220
  29.2 11.0 %copy-start.8 = (bf16[512,128]{1,0:T(8,128)(2,1)S(1)}, bf16[512,128]{1,0:T(8,128)(2,1)}, u32[]{:S(2)}) copy-start(bf16[512,128]{1,0:T(8,128)(2,1)} %param.12) | copy-start | bytes 393220
  30.1 24.9 %all-to-all-start.1 = ((bf16[32,64,128]{2,1,0:T(8,128)(2,1)}), bf16[32,64,128]{2,1,0:T(8,128)(2,1)S(1)}, u32[]{:S(2)}, u32[]{:S(2)}) async-start(bf16[32,64,128]{2,1,0:T(8,128)(2,1)} %bitcast.11), calls=%async_computation.1 | async-start | bytes 1048576 | tf_op jit(solution)/shard_map/all_to_all | solution.py:15
  59.9 30.3 %all-to-all-start = ((bf16[64,32,128]{2,1,0:T(8,128)(2,1)}), bf16[64,32,128]{2,1,0:T(8,128)(2,1)S(1)}, u32[]{:S(2)}, u32[]{:S(2)}) async-start(bf16[64,32,128]{2,1,0:T(8,128)(2,1)} %pad_maximum_fusion), calls=%async_computation | async-start | bytes 1048576 | tf_op jit(solution)/shard_map/all_to_all | solution.py:15
  90.1 38.9 %all-to-all-start.4 = ((bf16[64,8,8,128]{3,2,1,0:T(8,128)(2,1)}), bf16[64,8,8,128]{3,2,1,0:T(8,128)(2,1)S(1)}, u32[]{:S(2)}, u32[]{:S(2)}) async-start(bf16[64,8,8,128]{3,2,1,0:T(8,128)(2,1)} %copy.95), calls=%async_computation.4 | async-start | bytes 2097152 | tf_op jit(solution)/shard_map/all_to_all | solution.py:15
  133.9 1.2 copy-start.1
  140.1 0.9 copy-start.2
  141.9 1.0 copy-start.9
  142.1 0.9 copy-start.3

commit v2 on v1

v2 whole, which is shorter than its diff:
```python
import math

import jax
import jax.numpy as jnp
import numpy as np
from jax import lax
from jax.experimental import pallas as pl
from jax.experimental.pallas import tpu as pltpu
from jax.sharding import Mesh, PartitionSpec as P


SEQ = ("z", "x", "yh")
CH = ("yl", "core")
SPLIT = {"z": 8, "x": 4, "yh": 2, "yl": 4, "core": 2}
PARTS = ("x", "yh")
SHIFTS = (0, 1, 2, -1)
VMEM = pl.BlockSpec(memory_space=pltpu.VMEM)
INNER = 128
HALF = 64
LINES = 80


def swap(value, axes):
    return lax.all_to_all(value, axes, split_axis=0, concat_axis=0, tiled=True)


def flip(value, axis, bit):
    count = SPLIT[axis]
    return lax.ppermute(value, axis, [(i, i ^ bit) for i in range(count)])


def high_low(table):
    high = table.astype(jnp.bfloat16)
    low = (table - high.astype(np.float64)).astype(jnp.bfloat16)
    return high, low


def spectral_tables():
    total = 2 * HALF * INNER
    lines = np.arange(LINES)[:, None]
    kept = (lines <= HALF).astype(np.float64)
    weight = np.where((lines == 0) | (lines == HALF), 1.0, 2.0) * kept / total
    blocks = np.arange(HALF)[None, :]
    turn = 2.0 * math.pi * (lines * blocks % (2 * HALF)) / (2 * HALF)
    first = np.concatenate([np.cos(turn) * kept, -np.sin(turn) * kept])
    last = np.concatenate([np.cos(turn) * weight, -np.sin(turn) * weight]).T
    place = np.arange(INNER)
    twist = 2.0 * math.pi * (lines * place[None, :] % total) / total
    inner = 2.0 * math.pi * (place[:, None] * place[None, :] % INNER) / INNER
    cos_q, sin_q = np.cos(inner), np.sin(inner)
    middle = np.block([[cos_q, -sin_q], [sin_q, cos_q]])
    first_high, first_low = high_low(first)
    last_high, last_low = high_low(last)
    middle_high, middle_low = high_low(middle)
    return (
        np.concatenate([first_high, first_low], axis=1),
        np.concatenate([last_high, last_high, last_low], axis=1),
        middle_high,
        middle_low,
        np.cos(twist).astype(np.float32),
        np.sin(twist).astype(np.float32),
    )


def dot(first, second, first_dim=1, second_dim=0):
    return lax.dot_general(
        first,
        second,
        (((first_dim,), (second_dim,)), ((), ())),
        preferred_element_type=jnp.float32,
    )


def two_parts(value):
    high = value.astype(jnp.bfloat16)
    return high, (value - high.astype(jnp.float32)).astype(jnp.bfloat16)


def product(value, table_high, table_low, table_dim):
    high, low = two_parts(value)
    return (
        dot(high, table_high, 1, table_dim)
        + dot(high, table_low, 1, table_dim)
        + dot(low, table_high, 1, table_dim)
    )


def spectrum(rows_ref, items, first, middle_high, middle_low, cos_t, sin_t):
    series = jnp.concatenate(
        [rows_ref[pl.ds(c, HALF, stride=items), :] for c in range(items)], axis=1
    ).astype(jnp.bfloat16)
    lines = dot(first, jnp.concatenate([series, series], axis=0))
    turned = []
    for c in range(items):
        at = slice(c * INNER, (c + 1) * INNER)
        real, imag = lines[:LINES, at], lines[LINES:, at]
        turned.append(
            jnp.concatenate([real * cos_t + imag * sin_t, imag * cos_t - real * sin_t], axis=1)
        )
    return product(jnp.concatenate(turned, axis=0), middle_high, middle_low, 0)


def conv_kernel(
    scale,
    near,
    home_ref,
    taps_ref,
    back_taps_ref,
    first_ref,
    last_ref,
    high_ref,
    low_ref,
    cos_ref,
    sin_ref,
    out_ref,
    rows_ref,
    back_ref,
):
    count, inner = rows_ref.shape
    items = count // HALF
    parts = home_ref.shape[1] - 4
    first = first_ref[...]
    cos_t, sin_t = cos_ref[...], sin_ref[...]
    high, low = high_ref[...], low_ref[...]
    rows_ref[...] = home_ref[:, parts].astype(jnp.float32).reshape(count, inner)
    filt = spectrum(rows_ref, items, first, high, low, cos_t, sin_t)
    filt_re, filt_im = filt[:, :inner], filt[:, inner:]
    values = home_ref[:, parts + 2].astype(jnp.float32).reshape(count, inner)
    values = values.astype(jnp.bfloat16)
    before = dot(values, back_taps_ref[:, :inner], 1, 1)
    filtered = dot(values, back_taps_ref[:, inner:], 1, 1)
    filtered += jnp.concatenate([jnp.zeros((items, inner), jnp.float32), before[:-items]], axis=0)
    for block in range(HALF):
        far, rest = divmod(block, parts * near)
        shard, side = divmod(rest, near)
        total = home_ref[far * parts * near + side, shard].astype(jnp.float32)
        for p in range(1, parts):
            total += home_ref[(far * parts + p) * near + side, shard].astype(jnp.float32)
        gate = home_ref[block, parts + 3].astype(jnp.float32)
        total = (total * gate).astype(jnp.bfloat16)
        rows_ref[block * items : (block + 1) * items, :] = total.astype(jnp.float32)
    grad = spectrum(rows_ref, items, first, high, low, cos_t, sin_t)
    grad_re, grad_im = grad[:, :inner], grad[:, inner:]
    both = jnp.concatenate(
        [filt_re * grad_re + filt_im * grad_im, filt_re * grad_im - filt_im * grad_re], axis=1
    )
    both = product(both, high, low, 1)
    lines = []
    for c in range(items):
        at = slice(c * LINES, (c + 1) * LINES)
        real, imag = both[at, :inner], both[at, inner:]
        lines.append(
            jnp.concatenate([real * cos_t - imag * sin_t, imag * cos_t + real * sin_t], axis=0)
        )
    line_high, line_low = two_parts(jnp.concatenate(lines, axis=1))
    result = dot(last_ref[...], jnp.concatenate([line_high, line_low, line_high], axis=0))
    for c in range(items):
        back_ref[pl.ds(c, HALF, stride=items), :] = result[:, c * inner : (c + 1) * inner]
    d_w = back_ref[...].astype(jnp.bfloat16).astype(jnp.float32)
    d_key = d_w * filtered
    keys = home_ref[:, parts + 1].astype(jnp.float32).reshape(count, inner)
    d_vf = (d_w * keys).astype(jnp.bfloat16).astype(jnp.float32)
    ahead = jnp.concatenate([d_vf[items:], jnp.zeros((items, inner), jnp.float32)], axis=0)
    pair = jnp.concatenate([d_vf, ahead], axis=1).astype(jnp.bfloat16)
    d_value = dot(pair, taps_ref[...], 1, 1)
    corr = dot(pair, values, 0, 0)
    corr = jnp.concatenate([corr[inner:], corr[:inner]], axis=1)
    row = lax.broadcasted_iota(jnp.int32, corr.shape, 0)
    shift = 1
    while shift < inner:
        moved = pltpu.roll(corr, 2 * inner - shift, 1)
        corr = jnp.where((row & shift) != 0, moved, corr)
        shift *= 2
    sums = jnp.sum(corr, axis=0, keepdims=True) * scale
    sums = pltpu.roll(jnp.broadcast_to(sums, (16, 2 * inner)), 2 * inner - 1, 1)[:, :inner]
    sum_high = sums.astype(jnp.bfloat16).astype(jnp.float32)
    line = lax.broadcasted_iota(jnp.int32, sums.shape, 0)
    sums = jnp.where(line == 0, sum_high, jnp.where(line == 1, sums - sum_high, 0.0))
    across = lax.broadcasted_iota(jnp.int32, (inner, inner), 0)
    across = across + lax.broadcasted_iota(jnp.int32, (inner, inner), 1)
    mirror = jnp.where(across == inner - 1, 1.0, 0.0).astype(jnp.bfloat16)
    sums = dot(sums.astype(jnp.bfloat16), mirror)[:items]
    out_ref[:, 0:items, :] = d_key.reshape(HALF, items, inner).astype(jnp.bfloat16)
    out_ref[:, items : 2 * items, :] = d_value.reshape(HALF, items, inner).astype(jnp.bfloat16)
    out_ref[:, 2 * items :, :] = jnp.broadcast_to(sums[None], (HALF, items, inner)).astype(
        jnp.bfloat16
    )


def project_kernel(mine_ref, other_ref, *rest):
    block_refs, own_refs, (out_ref, held_ref) = rest[:4], rest[4:-2], rest[-2:]
    shards, lines, depth, rows = mine_ref.shape
    z, core = lax.axis_index("z"), lax.axis_index("core")
    for shift, block_ref in zip(SHIFTS, block_refs):
        for e in range(2):
            source = ((z - shift) & 7) ^ (4 * e)
            place = (source & 6) + ((source & 1) ^ core)
            at = pl.multiple_of(place * depth, depth)
            held_ref[pl.ds(at, depth), :] = block_ref[e]
    weight = held_ref[...].T
    dests = out_ref.shape[0]
    for i, own_ref in enumerate(own_refs):
        out_ref[:, shards + i] = own_ref[...]
    for s in range(0, shards, 2):
        columns = []
        for t in (s, s + 1):
            stack = []
            for y in range(lines):
                stack += [mine_ref[t, y], other_ref[t, y]]
            columns.append(jnp.concatenate(stack, axis=0))
        result = dot(weight, jnp.concatenate(columns, axis=1))
        for i, t in enumerate((s, s + 1)):
            piece = result[:, i * rows : (i + 1) * rows]
            out_ref[:, t] = piece.reshape(dests, -1, rows).astype(jnp.bfloat16)


def local(queries, key_feat, value_feat, out_grad, out_weight, long_filter, short_filter):
    channels, row_count = out_grad.shape
    group_count, tap_count = short_filter.shape
    per_group = channels // group_count
    split = math.prod(SPLIT[a] for a in PARTS)
    seq_devices = SPLIT["z"] * SPLIT["x"] * SPLIT["yh"]
    items = channels // seq_devices
    depth = channels // split

    count_z = SPLIT["z"]
    weight = out_weight.T
    opposite = flip(weight, "z", 4)
    blocks = [jnp.stack([weight, opposite])]
    for k in SHIFTS[1:]:
        ring = [(i, (i + k) % count_z) for i in range(count_z)]
        blocks.append(lax.ppermute(blocks[0], "z", ring))

    grad = out_grad.reshape(split, 1, depth, row_count)
    grad = jnp.broadcast_to(grad, (split, SPLIT["yl"], depth, row_count))
    grad = swap(grad.reshape(split * SPLIT["yl"], depth, row_count), PARTS + ("yl",))
    other = flip(grad, "core", 1)
    form = (split, SPLIT["yl"], depth, row_count)

    pieces = [
        a.reshape(seq_devices, items, row_count)
        for a in (long_filter, key_feat, value_feat, queries)
    ]
    partial = pl.pallas_call(
        project_kernel,
        out_shape=jax.ShapeDtypeStruct((seq_devices, split + 4, items, row_count), jnp.bfloat16),
        in_specs=[VMEM] * 10,
        out_specs=VMEM,
        scratch_shapes=[pltpu.VMEM((8 * depth, channels), jnp.bfloat16)],
        cost_estimate=pl.CostEstimate(
            flops=2 * channels * 8 * depth * split * row_count, bytes_accessed=3 << 20, transcendentals=0
        ),
        compiler_params=pltpu.CompilerParams(vmem_limit_bytes=24 << 20),
        name="project",
    )(grad.reshape(form), other.reshape(form), *blocks, *pieces)
    partial = swap(partial, SEQ)
    near = seq_devices // (SPLIT["z"] * split)
    near = seq_devices // (SPLIT["z"] * split)

    place = lax.axis_index(SEQ) * items // per_group
    taps = lax.dynamic_slice_in_dim(short_filter, place, 1, 0)
    padded = jnp.pad(taps[0], (0, tap_count + 1))
    toeplitz = jnp.tile(padded, tap_count)[: 2 * tap_count * tap_count]
    toeplitz = toeplitz.reshape(tap_count, 2 * tap_count)
    first, last, high, low, cos_t, sin_t = spectral_tables()
    count = seq_devices * items
    scale = 1.0 / math.sqrt(row_count * seq_devices * per_group)

    def conv(*refs):
        conv_kernel(scale, near, *refs)

    home = pl.pallas_call(
        conv,
        out_shape=jax.ShapeDtypeStruct((seq_devices, 3 * items, row_count), jnp.bfloat16),
        in_specs=[VMEM] * 9,
        out_specs=VMEM,
        scratch_shapes=[pltpu.VMEM((count, row_count), jnp.float32)] * 2,
        cost_estimate=pl.CostEstimate(flops=1 << 31, bytes_accessed=4 << 20, transcendentals=0),
        compiler_params=pltpu.CompilerParams(vmem_limit_bytes=24 << 20),
        name="conv",
    )(partial, toeplitz, toeplitz[::-1, ::-1], first, last, high, low, cos_t, sin_t)
    home = home.reshape(seq_devices, 3 * items // 2, 2, row_count)[:, : items + 1]
    home = swap(home, SEQ)
    d_key = home[:, : items // 2].reshape(seq_devices, items, row_count)
    d_value = home[:, items // 2 : items].reshape(seq_devices, items, row_count)
    both = home[:, items].astype(jnp.float32)
    both = both[:, 0] + both[:, 1]
    d_filter = jnp.sum(both.reshape(group_count, seq_devices // group_count, tap_count), axis=1)
    return (d_key.reshape(channels, row_count), d_value.reshape(channels, row_count), d_filter)


def solution(mesh):
    fine = Mesh(mesh.devices.reshape(tuple(SPLIT.values())), tuple(SPLIT))
    placed = (P(CH, SEQ),) * 6 + (P(CH, None),)

    return jax.shard_map(
        local,
        mesh=fine,
        in_specs=placed,
        out_specs=(P(CH, SEQ), P(CH, SEQ), P(CH, None)),
        check_vma=False,
    )
```

time: 169 us -> 145 us (0.86)
  matrix products: 19.3 us -> 0 us
  starting transfers between devices: 21.6 us -> 35.6 us
  waiting for transfers between devices: 59.8 us -> 50.7 us
  blocking collectives: 55.8 us -> 48.3 us
  local copies, waits for them, and re-layouts: 8.62 us -> 2.88 us
  Pallas kernels: 0 us -> 5.05 us
  other arithmetic: 2.49 us -> 0.72 us
    ppermute x0 -> x5, starting transfers between devices: none -> 25.6 us  [the longest x2 12.8 us: flip(): return lax.ppermute(value, axis, [(i, i ^ bit) for i in range(count)])]
    dot_general x22 -> x0, matrix products: 19.3 us -> none  [the longest x18 17.9 us: contract(): return jnp.einsum(form, first, second, precision=highest)]
    all_to_all x3 -> x1, waiting for transfers between devices: 59.8 us -> 43.9 us  [swap(): return lax.all_to_all(value, axes, split_axis=0, concat_axis=0, tiled=True)]
    all_to_all x3 -> x1, starting transfers between devices: 21.6 us -> 10.1 us  [swap(): return lax.all_to_all(value, axes, split_axis=0, concat_axis=0, tiled=True)]
    all_to_all x3 -> x2, blocking collectives: 55.8 us -> 48.3 us  [swap(): return lax.all_to_all(value, axes, split_axis=0, concat_axis=0, tiled=True)]
    ppermute x0 -> x5, waiting for transfers between devices: none -> 6.83 us  [the longest x3 3.99 us: local(): blocks.append(lax.ppermute(blocks[0], 'z', ring))]
    pallas_call x0 -> x2, Pallas kernels: none -> 5.05 us  [the longest x1 3.03 us: local(): pl.pallas_call(conv, out_shape=jax.ShapeDtypeStruct((seq_devices, 3 * ite...]
  transfers between devices with their start and end apart: 3 -> 6, of which waited for: 3 -> 4; matrix products, arithmetic and copies ran while one was open for 7% -> 0% of each run, Pallas kernels for 0% -> 0%
where the time goes in v2:
time: 145 us; the launch traced here: 144 us
  waiting for transfers between devices  50.7 us (35%)
  blocking collectives  48.3 us (33%)
  starting transfers between devices  35.6 us (25%)
  Pallas kernels  5.05 us (3%)
  local copies, waits for them, and re-layouts  2.88 us (2%)
    all_to_all x2, blocking collectives, swap(): return lax.all_to_all(value, axes, split_axis=0, concat_axis=0, tiled=True)  48.3 us
    all_to_all x1, waiting for transfers between devices, swap(): return lax.all_to_all(value, axes, split_axis=0, concat_axis=0, tiled=True)  43.9 us
    ppermute x2, starting transfers between devices, flip(): return lax.ppermute(value, axis, [(i, i ^ bit) for i in range(count)])  12.8 us
    ppermute x3, starting transfers between devices, local(): blocks.append(lax.ppermute(blocks[0], 'z', ring))  12.7 us
    all_to_all x1, starting transfers between devices, swap(): return lax.all_to_all(value, axes, split_axis=0, concat_axis=0, tiled=True)  10.1 us
    ppermute x3, waiting for transfers between devices, local(): blocks.append(lax.ppermute(blocks[0], 'z', ring))  3.99 us
    pallas_call x1, Pallas kernels, local(): pl.pallas_call(conv, out_shape=jax.ShapeDtypeStruct((seq_devices, 3 * ite...  3.03 us
  transfers between devices with their start and end apart: 6, of which 4 were waited for; matrix products, arithmetic and copies ran while one was open for 0% of the time, Pallas kernels for 0%

profile of v2, /device:TPU:16, one launch (start us, length us, event | category | flops | bytes accessed | tf_op | source)
XLA Modules:
  0.0 144.2 jit_solution(3099162666436641996)
XLA Ops:
  0.6 0.0 copy-start
  0.6 0.0 copy-start.11
  0.7 0.0 copy-start.1
  0.7 0.0 copy-start.2
  0.7 0.0 copy-start.3
  0.7 0.0 copy-start.4
  0.7 1.1 broadcast_in_dim.8
  1.8 26.5 %all_to_all.15 = bf16[32,64,128]{2,1,0:T(8,128)(2,1)S(1)} all-to-all(bf16[32,64,128]{2,1,0:T(8,128)(2,1)S(1)} %bitcast.30), channel_id=1, replica_groups=mesh['z'=8,'x'=4,'yh'=2,'yl'=4,'core'=2] {'x','yh','yl'}, dimensions={0} | all-to-all | bytes 1048576 | tf_op jit(solution)/shard_map/all_to_all | solution.py:24
  28.3 1.9 %collective-permute-start = (bf16[32,64,128]{2,1,0:T(8,128)(2,1)S(1)}, bf16[32,64,128]{2,1,0:T(8,128)(2,1)S(1)}, u32[]{:S(2)}, u32[]{:S(2)}) collective-permute-start(bf16[32,64,128]{2,1,0:T(8,128)(2,1)S(1)} %all_to_all.15), channel_id=1, source_target_pairs={{0,1},{1,0},{2,3},{3,2},{4,5},{5,4},{6,7},{7,6},{8,9},{9,8},{10,11... | collective-permute-start | bytes 1572872 | tf_op jit(solution)/shard_map/ppermute | solution.py:29
  30.2 0.0 copy-done.11
  30.2 10.9 %collective-permute-start.1 = (bf16[64,512]{1,0:T(8,128)(2,1)S(1)}, bf16[64,512]{1,0:T(8,128)(2,1)S(1)}, u32[]{:S(2)}, u32[]{:S(2)}) collective-permute-start(bf16[64,512]{1,0:T(8,128)(2,1)S(1)} %bitcast.35), channel_id=1, source_target_pairs={{0,256},{64,320},{128,384},{192,448},{256,0},{320,64},{384,128},{4... | collective-permute-start | bytes 196616 | tf_op jit(solution)/shard_map/ppermute | solution.py:29
  41.1 2.8 %collective-permute-done.1 = bf16[64,512]{1,0:T(8,128)(2,1)S(1)} collective-permute-done((bf16[64,512]{1,0:T(8,128)(2,1)S(1)}, bf16[64,512]{1,0:T(8,128)(2,1)S(1)}, u32[]{:S(2)}, u32[]{:S(2)}) %collective-permute-start.1) | collective-permute-done | bytes 65568 | tf_op jit(solution)/shard_map/ppermute | solution.py:29
  44.0 3.3 %collective-permute-start.2 = (bf16[2,64,512]{2,1,0:T(8,128)(2,1)S(1)}, bf16[2,64,512]{2,1,0:T(8,128)(2,1)S(1)}, u32[]{:S(2)}, u32[]{:S(2)}) collective-permute-start(bf16[2,64,512]{2,1,0:T(8,128)(2,1)S(1)} %pad_maximum_fusion.rest_0_), channel_id=1, source_target_pairs={{0,64},{64,128},{128,192},{192,256},{256,320},{320,384},{384,448},... | collective-permute-start | bytes 393224 | tf_op jit(solution)/shard_map/ppermute | solution.py:232
  47.2 4.3 %collective-permute-start.3 = (bf16[2,64,512]{2,1,0:T(8,128)(2,1)S(1)}, bf16[2,64,512]{2,1,0:T(8,128)(2,1)S(1)}, u32[]{:S(2)}, u32[]{:S(2)}) collective-permute-start(bf16[2,64,512]{2,1,0:T(8,128)(2,1)S(1)} %pad_maximum_fusion.rest_0_), channel_id=1, source_target_pairs={{0,128},{64,192},{128,256},{192,320},{256,384},{320,448},{384,0},{... | collective-permute-start | bytes 393224 | tf_op jit(solution)/shard_map/ppermute | solution.py:232
  51.6 5.1 %collective-permute-start.4 = (bf16[2,64,512]{2,1,0:T(8,128)(2,1)S(1)}, bf16[2,64,512]{2,1,0:T(8,128)(2,1)S(1)}, u32[]{:S(2)}, u32[]{:S(2)}) collective-permute-start(bf16[2,64,512]{2,1,0:T(8,128)(2,1)S(1)} %pad_maximum_fusion.rest_0_), channel_id=1, source_target_pairs={{0,448},{64,0},{128,64},{192,128},{256,192},{320,256},{384,320},{4... | collective-permute-start | bytes 393224 | tf_op jit(solution)/shard_map/ppermute | solution.py:232
  56.7 0.0 collective-permute-done.2.rest_1_
  56.7 3.0 %collective-permute-done.3.rest_2_ = bf16[2,64,512]{2,1,0:T(8,128)(2,1)S(1)} collective-permute-done((bf16[2,64,512]{2,1,0:T(8,128)(2,1)S(1)}, bf16[2,64,512]{2,1,0:T(8,128)(2,1)S(1)}, u32[]{:S(2)}, u32[]{:S(2)}) %collective-permute-start.3) | collective-permute-done | bytes 131104 | tf_op jit(solution)/shard_map/ppermute | solution.py:232
  59.7 1.0 collective-permute-done.4.rest_3_
  60.7 0.0 collective-permute-done
  60.7 2.0 %project.1 = bf16[64,12,8,128]{3,2,1,0:T(8,128)(2,1)} custom-call(bf16[8,4,64,128]{3,2,1,0:T(8,128)(2,1)S(1)} %bitcast.23, bf16[8,4,64,128]{3,2,1,0:T(8,128)(2,1)S(1)} %bitcast.24, bf16[2,64,512]{2,1,0:T(8,128)(2,1)S(1)} %pad_maximum_fusion.rest_0_, bf16[2,64,512]{2,1,0:T(8,128)(2,1)S(1)} %collective-permute-done.2.rest_1_, ...), custom_call_target="tpu_custom_call" | custom-call | flops 536870912 | bytes 3145728 | tf_op jit(solution)/shard_map/project/pallas_call | solution.py:244
  62.8 0.0 copy-start.9
  62.8 0.0 copy-start.10
  62.8 10.1 %all-to-all-start.1 = ((bf16[64,12,8,128]{3,2,1,0:T(8,128)(2,1)}), bf16[64,12,8,128]{3,2,1,0:T(8,128)(2,1)S(1)}, u32[]{:S(2)}, u32[]{:S(2)}) async-start(bf16[64,12,8,128]{3,2,1,0:T(8,128)(2,1)} %project.1), calls=%async_computation.1 | async-start | bytes 3145728 | tf_op jit(solution)/shard_map/all_to_all | solution.py:24
  73.0 0.3 tile.10
  73.3 0.2 rev.3.refs_2_
  73.6 43.9 %all-to-all-done.1.refs_0_ = bf16[64,12,8,128]{3,2,1,0:T(8,128)(2,1)S(1)} async-done(((bf16[64,12,8,128]{3,2,1,0:T(8,128)(2,1)}), bf16[64,12,8,128]{3,2,1,0:T(8,128)(2,1)S(1)}, u32[]{:S(2)}, u32[]{:S(2)}) %all-to-all-start.1) | async-done | bytes 1572896 | tf_op jit(solution)/shard_map/all_to_all | solution.py:24
  117.5 0.0 copy-done.6
  117.5 3.0 %conv.1 = bf16[64,24,128]{2,1,0:T(8,128)(2,1)S(1)} custom-call(bf16[64,12,8,128]{3,2,1,0:T(8,128)(2,1)S(1)} %all-to-all-done.1.refs_0_, bf16[128,256]{1,0:T(8,128)(2,1)S(1)} %reshape.49.refs_1_, bf16[128,256]{1,0:T(8,128)(2,1)S(1)} %rev.3.refs_2_, bf16[160,128]{1,0:T(8,128)(2,1)S(1)} %copy-done.8, bf16[64,480]{1,0:T(8,128)(2,1)S(1)} %copy-done.7, ...), custom_call_target="tpu_custom_call" | custom-call | flops 2147483648 | bytes 4194304 | tf_op jit(solution)/shard_map/conv/pallas_call | solution.py:272
  120.6 0.2 slice.29
  120.8 21.8 %all_to_all.16 = bf16[64,9,2,128]{3,2,1,0:T(2,128)(2,1)S(1)} all-to-all(bf16[64,9,2,128]{3,2,1,0:T(2,128)(2,1)S(1)} %slice.29), channel_id=1, replica_groups=mesh['z'=8,'x'=4,'yh'=2,'yl'=4,'core'=2] {'z','x','yh'}, dimensions={0} | all-to-all | bytes 589824 | tf_op jit(solution)/shard_map/all_to_all | solution.py:24
  142.7 0.6 reduce_sum.9
  143.3 0.9 fusion.1
  (22 shorter events, 0.2 us)
Async XLA Ops:
  0.6 72.3 %copy-start = (bf16[32,128]{1,0:T(8,128)(2,1)S(1)}, bf16[32,128]{1,0:T(8,128)(2,1)}, u32[]{:S(2)}) copy-start(bf16[32,128]{1,0:T(8,128)(2,1)} %param.19) | copy-start | bytes 24580
  0.6 29.5 %copy-start.11 = (bf16[512,64]{0,1:T(8,128)(2,1)S(1)}, bf16[512,64]{0,1:T(8,128)(2,1)}, u32[]{:S(2)}) copy-start(bf16[512,64]{0,1:T(8,128)(2,1)} %param.17) | copy-start | bytes 196612
  0.7 60.1 %copy-start.1 = (bf16[512,128]{1,0:T(8,128)(2,1)S(1)}, bf16[512,128]{1,0:T(8,128)(2,1)}, u32[]{:S(2)}) copy-start(bf16[512,128]{1,0:T(8,128)(2,1)} %param.18) | copy-start | bytes 393220
  0.7 60.1 %copy-start.2 = (bf16[512,128]{1,0:T(8,128)(2,1)S(1)}, bf16[512,128]{1,0:T(8,128)(2,1)}, u32[]{:S(2)}) copy-start(bf16[512,128]{1,0:T(8,128)(2,1)} %param.14) | copy-start | bytes 393220
  0.7 60.0 %copy-start.3 = (bf16[512,128]{1,0:T(8,128)(2,1)S(1)}, bf16[512,128]{1,0:T(8,128)(2,1)}, u32[]{:S(2)}) copy-start(bf16[512,128]{1,0:T(8,128)(2,1)} %param.15) | copy-start | bytes 393220
  0.7 60.0 %copy-start.4 = (bf16[512,128]{1,0:T(8,128)(2,1)S(1)}, bf16[512,128]{1,0:T(8,128)(2,1)}, u32[]{:S(2)}) copy-start(bf16[512,128]{1,0:T(8,128)(2,1)} %param.13) | copy-start | bytes 393220
  28.3 32.5 %collective-permute-start = (bf16[32,64,128]{2,1,0:T(8,128)(2,1)S(1)}, bf16[32,64,128]{2,1,0:T(8,128)(2,1)S(1)}, u32[]{:S(2)}, u32[]{:S(2)}) collective-permute-start(bf16[32,64,128]{2,1,0:T(8,128)(2,1)S(1)} %all_to_all.15), channel_id=1, source_target_pairs={{0,1},{1,0},{2,3},{3,2},{4,5},{5,4},{6,7},{7,6},{8,9},{9,8},{10,11... | collective-permute-start | bytes 1572872 | tf_op jit(solution)/shard_map/ppermute | solution.py:29
  30.2 13.8 %collective-permute-start.1 = (bf16[64,512]{1,0:T(8,128)(2,1)S(1)}, bf16[64,512]{1,0:T(8,128)(2,1)S(1)}, u32[]{:S(2)}, u32[]{:S(2)}) collective-permute-start(bf16[64,512]{1,0:T(8,128)(2,1)S(1)} %bitcast.35), channel_id=1, source_target_pairs={{0,256},{64,320},{128,384},{192,448},{256,0},{320,64},{384,128},{4... | collective-permute-start | bytes 196616 | tf_op jit(solution)/shard_map/ppermute | solution.py:29
  44.0 12.8 %collective-permute-start.2 = (bf16[2,64,512]{2,1,0:T(8,128)(2,1)S(1)}, bf16[2,64,512]{2,1,0:T(8,128)(2,1)S(1)}, u32[]{:S(2)}, u32[]{:S(2)}) collective-permute-start(bf16[2,64,512]{2,1,0:T(8,128)(2,1)S(1)} %pad_maximum_fusion.rest_0_), channel_id=1, source_target_pairs={{0,64},{64,128},{128,192},{192,256},{256,320},{320,384},{384,448},... | collective-permute-start | bytes 393224 | tf_op jit(solution)/shard_map/ppermute | solution.py:232
  47.2 12.5 %collective-permute-start.3 = (bf16[2,64,512]{2,1,0:T(8,128)(2,1)S(1)}, bf16[2,64,512]{2,1,0:T(8,128)(2,1)S(1)}, u32[]{:S(2)}, u32[]{:S(2)}) collective-permute-start(bf16[2,64,512]{2,1,0:T(8,128)(2,1)S(1)} %pad_maximum_fusion.rest_0_), channel_id=1, source_target_pairs={{0,128},{64,192},{128,256},{192,320},{256,384},{320,448},{384,0},{... | collective-permute-start | bytes 393224 | tf_op jit(solution)/shard_map/ppermute | solution.py:232
  51.6 9.1 %collective-permute-start.4 = (bf16[2,64,512]{2,1,0:T(8,128)(2,1)S(1)}, bf16[2,64,512]{2,1,0:T(8,128)(2,1)S(1)}, u32[]{:S(2)}, u32[]{:S(2)}) collective-permute-start(bf16[2,64,512]{2,1,0:T(8,128)(2,1)S(1)} %pad_maximum_fusion.rest_0_), channel_id=1, source_target_pairs={{0,448},{64,0},{128,64},{192,128},{256,192},{320,256},{384,320},{4... | collective-permute-start | bytes 393224 | tf_op jit(solution)/shard_map/ppermute | solution.py:232
  62.8 54.7 %copy-start.5 = (bf16[256,256]{1,0:T(8,128)(2,1)S(1)}, bf16[256,256]{1,0:T(8,128)(2,1)}, u32[]{:S(2)}) copy-start(bf16[256,256]{1,0:T(8,128)(2,1)} %constant.57.clone.refs_5_) | copy-start | bytes 393220
  62.8 54.7 %copy-start.6 = (bf16[256,256]{1,0:T(8,128)(2,1)S(1)}, bf16[256,256]{1,0:T(8,128)(2,1)}, u32[]{:S(2)}) copy-start(bf16[256,256]{1,0:T(8,128)(2,1)} %constant.58.clone.refs_6_) | copy-start | bytes 393220
  62.8 54.7 %copy-start.7 = (bf16[64,480]{1,0:T(8,128)(2,1)S(1)}, bf16[64,480]{1,0:T(8,128)(2,1)}, u32[]{:S(2)}) copy-start(bf16[64,480]{1,0:T(8,128)(2,1)} %constant.56.clone.refs_4_) | copy-start | bytes 184324
  62.8 54.7 %copy-start.8 = (bf16[160,128]{1,0:T(8,128)(2,1)S(1)}, bf16[160,128]{1,0:T(8,128)(2,1)}, u32[]{:S(2)}) copy-start(bf16[160,128]{1,0:T(8,128)(2,1)} %constant.55.clone.refs_3_) | copy-start | bytes 122884
  62.8 54.7 %copy-start.9 = (f32[80,128]{1,0:T(8,128)S(1)}, f32[80,128]{1,0:T(8,128)}, u32[]{:S(2)}) copy-start(f32[80,128]{1,0:T(8,128)} %constant.59.clone.refs_7_) | copy-start | bytes 122884
  62.8 54.7 %copy-start.10 = (f32[80,128]{1,0:T(8,128)S(1)}, f32[80,128]{1,0:T(8,128)}, u32[]{:S(2)}) copy-start(f32[80,128]{1,0:T(8,128)} %constant.60.clone.refs_8_) | copy-start | bytes 122884
  62.8 54.7 %all-to-all-start.1 = ((bf16[64,12,8,128]{3,2,1,0:T(8,128)(2,1)}), bf16[64,12,8,128]{3,2,1,0:T(8,128)(2,1)S(1)}, u32[]{:S(2)}, u32[]{:S(2)}) async-start(bf16[64,12,8,128]{3,2,1,0:T(8,128)(2,1)} %project.1), calls=%async_computation.1 | async-start | bytes 3145728 | tf_op jit(solution)/shard_map/all_to_all | solution.py:24

commit v3 on v2

--- a/solution.py
+++ b/solution.py
@@ -12,12 +12,12 @@
 SEQ = ("z", "x", "yh")
 CH = ("yl", "core")
 SPLIT = {"z": 8, "x": 4, "yh": 2, "yl": 4, "core": 2}
-PARTS = ("x", "yh")
-SHIFTS = (0, 1, 2, -1)
+PARTS = ("x",)
+SHIFTS = (0, 2, -1, 1)
 VMEM = pl.BlockSpec(memory_space=pltpu.VMEM)
 INNER = 128
 HALF = 64
-LINES = 80
+LINES = 72
 
 
 def swap(value, axes):
@@ -118,27 +118,37 @@
 ):
     count, inner = rows_ref.shape
     items = count // HALF
-    parts = home_ref.shape[1] - 4
+    parts = home_ref.shape[1] // items - 4
+    shards = parts
+
+    def two(place):
+        both = home_ref[:, place * items : (place + 2) * items].astype(jnp.float32)
+        return [half.reshape(count, inner) for half in (both[:, :items], both[:, items:])]
+
+    filters, keys = two(shards)
+    values, gates = two(shards + 2)
     first = first_ref[...]
     cos_t, sin_t = cos_ref[...], sin_ref[...]
     high, low = high_ref[...], low_ref[...]
-    rows_ref[...] = home_ref[:, parts].astype(jnp.float32).reshape(count, inner)
+    rows_ref[...] = filters
     filt = spectrum(rows_ref, items, first, high, low, cos_t, sin_t)
     filt_re, filt_im = filt[:, :inner], filt[:, inner:]
-    values = home_ref[:, parts + 2].astype(jnp.float32).reshape(count, inner)
     values = values.astype(jnp.bfloat16)
     before = dot(values, back_taps_ref[:, :inner], 1, 1)
     filtered = dot(values, back_taps_ref[:, inner:], 1, 1)
     filtered += jnp.concatenate([jnp.zeros((items, inner), jnp.float32), before[:-items]], axis=0)
-    for block in range(HALF):
-        far, rest = divmod(block, parts * near)
-        shard, side = divmod(rest, near)
-        total = home_ref[far * parts * near + side, shard].astype(jnp.float32)
-        for p in range(1, parts):
-            total += home_ref[(far * parts + p) * near + side, shard].astype(jnp.float32)
-        gate = home_ref[block, parts + 3].astype(jnp.float32)
-        total = (total * gate).astype(jnp.bfloat16)
-        rows_ref[block * items : (block + 1) * items, :] = total.astype(jnp.float32)
+    for far in range(HALF // (parts * near)):
+        for side in range(near):
+            for shard in range(0, shards, 2):
+                at = slice(shard * items, (shard + 2) * items)
+                total = home_ref[far * parts * near + side, at].astype(jnp.float32)
+                for p in range(1, parts):
+                    total += home_ref[(far * parts + p) * near + side, at].astype(jnp.float32)
+                for i in range(2):
+                    block = (far * shards + shard + i) * near + side
+                    at = slice(block * items, (block + 1) * items)
+                    piece = (total[i * items : (i + 1) * items] * gates[at]).astype(jnp.bfloat16)
+                    rows_ref[at] = piece.astype(jnp.float32)
     grad = spectrum(rows_ref, items, first, high, low, cos_t, sin_t)
     grad_re, grad_im = grad[:, :inner], grad[:, inner:]
     both = jnp.concatenate(
@@ -158,7 +168,6 @@
         back_ref[pl.ds(c, HALF, stride=items), :] = result[:, c * inner : (c + 1) * inner]
     d_w = back_ref[...].astype(jnp.bfloat16).astype(jnp.float32)
     d_key = d_w * filtered
-    keys = home_ref[:, parts + 1].astype(jnp.float32).reshape(count, inner)
     d_vf = (d_w * keys).astype(jnp.bfloat16).astype(jnp.float32)
     ahead = jnp.concatenate([d_vf[items:], jnp.zeros((items, inner), jnp.float32)], axis=0)
     pair = jnp.concatenate([d_vf, ahead], axis=1).astype(jnp.bfloat16)
@@ -180,8 +189,8 @@
     across = across + lax.broadcasted_iota(jnp.int32, (inner, inner), 1)
     mirror = jnp.where(across == inner - 1, 1.0, 0.0).astype(jnp.bfloat16)
     sums = dot(sums.astype(jnp.bfloat16), mirror)[:items]
-    out_ref[:, 0:items, :] = d_key.reshape(HALF, items, inner).astype(jnp.bfloat16)
-    out_ref[:, items : 2 * items, :] = d_value.reshape(HALF, items, inner).astype(jnp.bfloat16)
+    both = [d_key.reshape(HALF, items, inner), d_value.reshape(HALF, items, inner)]
+    out_ref[:, 0 : 2 * items, :] = jnp.concatenate(both, axis=1).astype(jnp.bfloat16)
     out_ref[:, 2 * items :, :] = jnp.broadcast_to(sums[None], (HALF, items, inner)).astype(
         jnp.bfloat16
     )
@@ -189,18 +198,24 @@
 
 def project_kernel(mine_ref, other_ref, *rest):
     block_refs, own_refs, (out_ref, held_ref) = rest[:4], rest[4:-2], rest[-2:]
-    shards, lines, depth, rows = mine_ref.shape
-    z, core = lax.axis_index("z"), lax.axis_index("core")
+    shards, lines, _, rows = mine_ref.shape
+    z, core, yh = lax.axis_index("z"), lax.axis_index("core"), lax.axis_index("yh")
+    features = block_refs[0].shape[1]
     for shift, block_ref in zip(SHIFTS, block_refs):
-        for e in range(2):
-            source = ((z - shift) & 7) ^ (4 * e)
+        for e in range(4):
+            source = ((z - shift) & 7) ^ (4 * (e // 2))
+            if shift == 2:
+                source = source ^ (4 * (z & 1))
             place = (source & 6) + ((source & 1) ^ core)
-            at = pl.multiple_of(place * depth, depth)
-            held_ref[pl.ds(at, depth), :] = block_ref[e]
+            at = pl.multiple_of((2 * place + (yh ^ (e % 2))) * features, features)
+            held_ref[pl.ds(at, features), :] = block_ref[e]
     weight = held_ref[...].T
     dests = out_ref.shape[0]
-    for i, own_ref in enumerate(own_refs):
-        out_ref[:, shards + i] = own_ref[...]
+    items = out_ref.shape[1] // (shards + len(own_refs))
+    for i in range(0, len(own_refs), 2):
+        both = [own_ref[...].astype(jnp.float32) for own_ref in own_refs[i : i + 2]]
+        at = slice((shards + i) * items, (shards + i + 2) * items)
+        out_ref[:, at] = jnp.concatenate(both, axis=1).astype(jnp.bfloat16)
     for s in range(0, shards, 2):
         columns = []
         for t in (s, s + 1):
@@ -209,9 +224,14 @@
                 stack += [mine_ref[t, y], other_ref[t, y]]
             columns.append(jnp.concatenate(stack, axis=0))
         result = dot(weight, jnp.concatenate(columns, axis=1))
-        for i, t in enumerate((s, s + 1)):
-            piece = result[:, i * rows : (i + 1) * rows]
-            out_ref[:, t] = piece.reshape(dests, -1, rows).astype(jnp.bfloat16)
+        both = [result[:, at : at + rows].reshape(dests, items, rows) for at in (0, rows)]
+        at = slice(s * items, (s + 2) * items)
+        out_ref[:, at] = jnp.concatenate(both, axis=1).astype(jnp.bfloat16)
+
+
+def repeat_kernel(grad_ref, out_ref):
+    for y in range(out_ref.shape[1]):
+        out_ref[:, y] = grad_ref[...]
 
 
 def local(queries, key_feat, value_feat, out_grad, out_weight, long_filter, short_filter):
@@ -225,14 +245,23 @@
 
     count_z = SPLIT["z"]
     weight = out_weight.T
-    opposite = flip(weight, "z", 4)
-    blocks = [jnp.stack([weight, opposite])]
+    beside = flip(weight, "yh", 1)
+    pair = jnp.stack([weight, beside])
+    opposite = flip(pair, "z", 4)
+    blocks = [jnp.concatenate([pair, opposite])]
     for k in SHIFTS[1:]:
-        ring = [(i, (i + k) % count_z) for i in range(count_z)]
+        turn = [(-k if k == 2 and i % 2 else k) for i in range(count_z)]
+        ring = [(i, (i + turn[i]) % count_z) for i in range(count_z)]
         blocks.append(lax.ppermute(blocks[0], "z", ring))
 
-    grad = out_grad.reshape(split, 1, depth, row_count)
-    grad = jnp.broadcast_to(grad, (split, SPLIT["yl"], depth, row_count))
+    grad = pl.pallas_call(
+        repeat_kernel,
+        out_shape=jax.ShapeDtypeStruct((split, SPLIT["yl"], depth, row_count), jnp.bfloat16),
+        in_specs=[VMEM],
+        out_specs=VMEM,
+        compiler_params=pltpu.CompilerParams(vmem_limit_bytes=4 << 20),
+        name="repeat",
+    )(out_grad.reshape(split, depth, row_count))
     grad = swap(grad.reshape(split * SPLIT["yl"], depth, row_count), PARTS + ("yl",))
     other = flip(grad, "core", 1)
     form = (split, SPLIT["yl"], depth, row_count)
@@ -243,7 +272,7 @@
     ]
     partial = pl.pallas_call(
         project_kernel,
-        out_shape=jax.ShapeDtypeStruct((seq_devices, split + 4, items, row_count), jnp.bfloat16),
+        out_shape=jax.ShapeDtypeStruct((seq_devices, (split + 4) * items, row_count), jnp.bfloat16),
         in_specs=[VMEM] * 10,
         out_specs=VMEM,
         scratch_shapes=[pltpu.VMEM((8 * depth, channels), jnp.bfloat16)],

time: 145 us -> 139 us (0.959)
  the two profiles are of different devices: /device:TPU:16 before, /device:TPU:8 now
where the time goes in v3:
time: 139 us
  waiting for transfers between devices  58.3 us (42%)
  starting transfers between devices  48.7 us (35%)
  blocking collectives  21.9 us (16%)
  Pallas kernels  5.51 us (4%)
  local copies, waits for them, and re-layouts  2.72 us (2%)
    all_to_all x2, waiting for transfers between devices, swap(): return lax.all_to_all(value, axes, split_axis=0, concat_axis=0, tiled=True)  45.6 us
    all_to_all x1, blocking collectives, swap(): return lax.all_to_all(value, axes, split_axis=0, concat_axis=0, tiled=True)  21.9 us
    all_to_all x2, starting transfers between devices, swap(): return lax.all_to_all(value, axes, split_axis=0, concat_axis=0, tiled=True)  17.5 us
    ppermute x3, starting transfers between devices, flip(): return lax.ppermute(value, axis, [(i, i ^ bit) for i in range(count)])  16.6 us
    ppermute x3, starting transfers between devices, local(): blocks.append(lax.ppermute(blocks[0], 'z', ring))  14.6 us
    ppermute x3, waiting for transfers between devices, local(): blocks.append(lax.ppermute(blocks[0], 'z', ring))  8.45 us
    ppermute x3, waiting for transfers between devices, flip(): return lax.ppermute(value, axis, [(i, i ^ bit) for i in range(count)])  4.25 us
    pallas_call x1, Pallas kernels, local(): pl.pallas_call(conv, out_shape=jax.ShapeDtypeStruct((seq_devices, 3 * ite...  2.8 us
  transfers between devices with their start and end apart: 8, of which 6 were waited for; matrix products, arithmetic and copies ran while one was open for 0% of the time, Pallas kernels for 0%

profile of v3, /device:TPU:8, one launch (start us, length us, event | category | flops | bytes accessed | tf_op | source)
XLA Modules:
  0.0 138.9 jit_solution(9152799346866605928)
XLA Ops:
  0.6 0.0 copy-start
  0.7 0.9 copy-done.1
  1.6 0.9 repeat.1
  2.4 9.3 %all-to-all-start = ((bf16[16,128,128]{2,1,0:T(8,128)(2,1)}), bf16[16,128,128]{2,1,0:T(8,128)(2,1)S(1)}, u32[]{:S(2)}, u32[]{:S(2)}) async-start(bf16[16,128,128]{2,1,0:T(8,128)(2,1)} %bitcast.1), calls=%async_computation | async-start | bytes 1048576 | tf_op jit(solution)/shard_map/all_to_all | solution.py:24
  11.7 3.7 %collective-permute-start.1 = (bf16[64,512]{1,0:T(8,128)(2,1)S(1)}, bf16[64,512]{1,0:T(8,128)(2,1)S(1)}, u32[]{:S(2)}, u32[]{:S(2)}) collective-permute-start(bf16[64,512]{1,0:T(8,128)(2,1)S(1)} %bitcast.31), channel_id=1, source_target_pairs={{0,8},{8,0},{1,9},{9,1},{2,10},{10,2},{3,11},{11,3},{4,12},{12,4},... | collective-permute-start | bytes 196616 | tf_op jit(solution)/shard_map/ppermute | solution.py:29
  15.4 12.1 %all-to-all-done = bf16[16,128,128]{2,1,0:T(8,128)(2,1)S(1)} async-done(((bf16[16,128,128]{2,1,0:T(8,128)(2,1)}), bf16[16,128,128]{2,1,0:T(8,128)(2,1)S(1)}, u32[]{:S(2)}, u32[]{:S(2)}) %all-to-all-start) | async-done | bytes 524320 | tf_op jit(solution)/shard_map/all_to_all | solution.py:24
  27.6 1.9 %collective-permute-start = (bf16[16,128,128]{2,1,0:T(8,128)(2,1)S(1)}, bf16[16,128,128]{2,1,0:T(8,128)(2,1)S(1)}, u32[]{:S(2)}, u32[]{:S(2)}) collective-permute-start(bf16[16,128,128]{2,1,0:T(8,128)(2,1)S(1)} %all-to-all-done), channel_id=1, source_target_pairs={{0,1},{1,0},{2,3},{3,2},{4,5},{5,4},{6,7},{7,6},{8,9},{9,8},{10,11... | collective-permute-start | bytes 1572872 | tf_op jit(solution)/shard_map/ppermute | solution.py:29
  29.5 0.0 copy-start.2
  29.6 11.0 %collective-permute-start.2 = (bf16[2,64,512]{2,1,0:T(8,128)(2,1)S(1)}, bf16[2,64,512]{2,1,0:T(8,128)(2,1)S(1)}, u32[]{:S(2)}, u32[]{:S(2)}) collective-permute-start(bf16[2,64,512]{2,1,0:T(8,128)(2,1)S(1)} %pad_maximum_fusion.1), channel_id=1, source_target_pairs={{0,256},{64,320},{128,384},{192,448},{256,0},{320,64},{384,128},{4... | collective-permute-start | bytes 393224 | tf_op jit(solution)/shard_map/ppermute | solution.py:29
  40.5 4.2 %collective-permute-done.2 = bf16[2,64,512]{2,1,0:T(8,128)(2,1)S(1)} collective-permute-done((bf16[2,64,512]{2,1,0:T(8,128)(2,1)S(1)}, bf16[2,64,512]{2,1,0:T(8,128)(2,1)S(1)}, u32[]{:S(2)}, u32[]{:S(2)}) %collective-permute-start.2) | collective-permute-done | bytes 131104 | tf_op jit(solution)/shard_map/ppermute | solution.py:29
  44.8 7.1 %collective-permute-start.3 = (bf16[4,64,512]{2,1,0:T(8,128)(2,1)S(1)}, bf16[4,64,512]{2,1,0:T(8,128)(2,1)S(1)}, u32[]{:S(2)}, u32[]{:S(2)}) collective-permute-start(bf16[4,64,512]{2,1,0:T(8,128)(2,1)S(1)} %pad_maximum_fusion.rest_0_), channel_id=1, source_target_pairs={{0,128},{64,448},{128,256},{192,64},{256,384},{320,192},{384,0},{4... | collective-permute-start | bytes 786440 | tf_op jit(solution)/shard_map/ppermute | solution.py:255
  51.9 5.6 %collective-permute-start.4 = (bf16[4,64,512]{2,1,0:T(8,128)(2,1)S(1)}, bf16[4,64,512]{2,1,0:T(8,128)(2,1)S(1)}, u32[]{:S(2)}, u32[]{:S(2)}) collective-permute-start(bf16[4,64,512]{2,1,0:T(8,128)(2,1)S(1)} %pad_maximum_fusion.rest_0_), channel_id=1, source_target_pairs={{0,448},{64,0},{128,64},{192,128},{256,192},{320,256},{384,320},{4... | collective-permute-start | bytes 786440 | tf_op jit(solution)/shard_map/ppermute | solution.py:255
  57.5 1.9 %collective-permute-start.5 = (bf16[4,64,512]{2,1,0:T(8,128)(2,1)S(1)}, bf16[4,64,512]{2,1,0:T(8,128)(2,1)S(1)}, u32[]{:S(2)}, u32[]{:S(2)}) collective-permute-start(bf16[4,64,512]{2,1,0:T(8,128)(2,1)S(1)} %pad_maximum_fusion.rest_0_), channel_id=1, source_target_pairs={{0,64},{64,128},{128,192},{192,256},{256,320},{320,384},{384,448},... | collective-permute-start | bytes 786440 | tf_op jit(solution)/shard_map/ppermute | solution.py:255
  59.4 2.3 %collective-permute-done.3.rest_1_ = bf16[4,64,512]{2,1,0:T(8,128)(2,1)S(1)} collective-permute-done((bf16[4,64,512]{2,1,0:T(8,128)(2,1)S(1)}, bf16[4,64,512]{2,1,0:T(8,128)(2,1)S(1)}, u32[]{:S(2)}, u32[]{:S(2)}) %collective-permute-start.3) | collective-permute-done | bytes 262176 | tf_op jit(solution)/shard_map/ppermute | solution.py:255
  61.7 3.5 %collective-permute-done.4.rest_2_ = bf16[4,64,512]{2,1,0:T(8,128)(2,1)S(1)} collective-permute-done((bf16[4,64,512]{2,1,0:T(8,128)(2,1)S(1)}, bf16[4,64,512]{2,1,0:T(8,128)(2,1)S(1)}, u32[]{:S(2)}, u32[]{:S(2)}) %collective-permute-start.4) | collective-permute-done | bytes 262176 | tf_op jit(solution)/shard_map/ppermute | solution.py:255
  65.2 2.7 %collective-permute-done.5.rest_3_ = bf16[4,64,512]{2,1,0:T(8,128)(2,1)S(1)} collective-permute-done((bf16[4,64,512]{2,1,0:T(8,128)(2,1)S(1)}, bf16[4,64,512]{2,1,0:T(8,128)(2,1)S(1)}, u32[]{:S(2)}, u32[]{:S(2)}) %collective-permute-start.5) | collective-permute-done | bytes 262176 | tf_op jit(solution)/shard_map/ppermute | solution.py:255
  67.9 1.8 %project.1 = bf16[64,64,128]{2,1,0:T(8,128)(2,1)} custom-call(bf16[4,4,128,128]{3,2,1,0:T(8,128)(2,1)S(1)} %bitcast.23, bf16[4,4,128,128]{3,2,1,0:T(8,128)(2,1)S(1)} %bitcast.24, bf16[4,64,512]{2,1,0:T(8,128)(2,1)S(1)} %pad_maximum_fusion.rest_0_, bf16[4,64,512]{2,1,0:T(8,128)(2,1)S(1)} %collective-permute-done.3.rest_1_, ...), custom_call_target="tpu_custom_call" | custom-call | flops 536870912 | bytes 3145728 | tf_op jit(solution)/shard_map/project/pallas_call | solution.py:273
  69.8 8.2 %all-to-all-start.1 = ((bf16[64,64,128]{2,1,0:T(8,128)(2,1)}), bf16[64,64,128]{2,1,0:T(8,128)(2,1)S(1)}, u32[]{:S(2)}, u32[]{:S(2)}) async-start(bf16[64,64,128]{2,1,0:T(8,128)(2,1)} %project.1), calls=%async_computation.1 | async-start | bytes 2097152 | tf_op jit(solution)/shard_map/all_to_all | solution.py:24
  78.1 0.0 copy-start.10
  78.1 0.0 copy-start.11
  78.1 0.3 tile.10
  78.5 0.0 copy-start.8
  78.5 0.0 copy-start.9
  78.5 0.0 copy-start.6
  78.5 0.0 copy-start.7
  78.6 0.2 rev.3.refs_2_
  78.8 33.5 %all-to-all-done.1.refs_0_ = bf16[64,64,128]{2,1,0:T(8,128)(2,1)S(1)} async-done(((bf16[64,64,128]{2,1,0:T(8,128)(2,1)}), bf16[64,64,128]{2,1,0:T(8,128)(2,1)S(1)}, u32[]{:S(2)}, u32[]{:S(2)}) %all-to-all-start.1) | async-done | bytes 1048608 | tf_op jit(solution)/shard_map/all_to_all | solution.py:24
  112.3 2.8 %conv.1 = bf16[64,24,128]{2,1,0:T(8,128)(2,1)S(1)} custom-call(bf16[64,64,128]{2,1,0:T(8,128)(2,1)S(1)} %all-to-all-done.1.refs_0_, bf16[128,256]{1,0:T(8,128)(2,1)S(1)} %reshape.51.refs_1_, bf16[128,256]{1,0:T(8,128)(2,1)S(1)} %rev.3.refs_2_, bf16[144,128]{1,0:T(8,128)(2,1)S(1)} %copy-done.9, bf16[64,432]{1,0:T(8,128)(2,1)S(1)} %copy-done.8, ...), custom_call_target="tpu_custom_call" | custom-call | flops 2147483648 | bytes 4194304 | tf_op jit(solution)/shard_map/conv/pallas_call | solution.py:301
  115.2 0.2 slice.29
  115.4 21.9 %all_to_all.15 = bf16[64,9,2,128]{3,2,1,0:T(2,128)(2,1)S(1)} all-to-all(bf16[64,9,2,128]{3,2,1,0:T(2,128)(2,1)S(1)} %slice.29), channel_id=1, replica_groups=mesh['z'=8,'x'=4,'yh'=2,'yl'=4,'core'=2] {'z','x','yh'}, dimensions={0} | all-to-all | bytes 589824 | tf_op jit(solution)/shard_map/all_to_all | solution.py:24
  137.4 0.6 reduce_sum.9
  138.0 0.9 fusion.1
  (28 shorter events, 0.2 us)
Async XLA Ops:
  0.6 77.4 %copy-start = (bf16[32,128]{1,0:T(8,128)(2,1)S(1)}, bf16[32,128]{1,0:T(8,128)(2,1)}, u32[]{:S(2)}) copy-start(bf16[32,128]{1,0:T(8,128)(2,1)} %param.19) | copy-start | bytes 24580
  0.6 0.9 copy-start.1
  2.4 9.3 %copy-start.12 = (bf16[512,64]{0,1:T(8,128)(2,1)S(1)}, bf16[512,64]{0,1:T(8,128)(2,1)}, u32[]{:S(2)}) copy-start(bf16[512,64]{0,1:T(8,128)(2,1)} %param.17) | copy-start | bytes 196612
  2.4 25.1 %all-to-all-start = ((bf16[16,128,128]{2,1,0:T(8,128)(2,1)}), bf16[16,128,128]{2,1,0:T(8,128)(2,1)S(1)}, u32[]{:S(2)}, u32[]{:S(2)}) async-start(bf16[16,128,128]{2,1,0:T(8,128)(2,1)} %bitcast.1), calls=%async_computation | async-start | bytes 1048576 | tf_op jit(solution)/shard_map/all_to_all | solution.py:24
  11.7 17.7 %collective-permute-start.1 = (bf16[64,512]{1,0:T(8,128)(2,1)S(1)}, bf16[64,512]{1,0:T(8,128)(2,1)S(1)}, u32[]{:S(2)}, u32[]{:S(2)}) collective-permute-start(bf16[64,512]{1,0:T(8,128)(2,1)S(1)} %bitcast.31), channel_id=1, source_target_pairs={{0,8},{8,0},{1,9},{9,1},{2,10},{10,2},{3,11},{11,3},{4,12},{12,4},... | collective-permute-start | bytes 196616 | tf_op jit(solution)/shard_map/ppermute | solution.py:29
  27.6 40.4 %collective-permute-start = (bf16[16,128,128]{2,1,0:T(8,128)(2,1)S(1)}, bf16[16,128,128]{2,1,0:T(8,128)(2,1)S(1)}, u32[]{:S(2)}, u32[]{:S(2)}) collective-permute-start(bf16[16,128,128]{2,1,0:T(8,128)(2,1)S(1)} %all-to-all-done), channel_id=1, source_target_pairs={{0,1},{1,0},{2,3},{3,2},{4,5},{5,4},{6,7},{7,6},{8,9},{9,8},{10,11... | collective-permute-start | bytes 1572872 | tf_op jit(solution)/shard_map/ppermute | solution.py:29
  29.5 38.4 %copy-start.2 = (bf16[512,128]{1,0:T(8,128)(2,1)S(1)}, bf16[512,128]{1,0:T(8,128)(2,1)}, u32[]{:S(2)}) copy-start(bf16[512,128]{1,0:T(8,128)(2,1)} %param.18) | copy-start | bytes 393220
  29.5 38.4 %copy-start.3 = (bf16[512,128]{1,0:T(8,128)(2,1)S(1)}, bf16[512,128]{1,0:T(8,128)(2,1)}, u32[]{:S(2)}) copy-start(bf16[512,128]{1,0:T(8,128)(2,1)} %param.14) | copy-start | bytes 393220
  29.5 38.4 %copy-start.4 = (bf16[512,128]{1,0:T(8,128)(2,1)S(1)}, bf16[512,128]{1,0:T(8,128)(2,1)}, u32[]{:S(2)}) copy-start(bf16[512,128]{1,0:T(8,128)(2,1)} %param.15) | copy-start | bytes 393220
  29.5 38.4 %copy-start.5 = (bf16[512,128]{1,0:T(8,128)(2,1)S(1)}, bf16[512,128]{1,0:T(8,128)(2,1)}, u32[]{:S(2)}) copy-start(bf16[512,128]{1,0:T(8,128)(2,1)} %param.13) | copy-start | bytes 393220
  29.6 15.2 %collective-permute-start.2 = (bf16[2,64,512]{2,1,0:T(8,128)(2,1)S(1)}, bf16[2,64,512]{2,1,0:T(8,128)(2,1)S(1)}, u32[]{:S(2)}, u32[]{:S(2)}) collective-permute-start(bf16[2,64,512]{2,1,0:T(8,128)(2,1)S(1)} %pad_maximum_fusion.1), channel_id=1, source_target_pairs={{0,256},{64,320},{128,384},{192,448},{256,0},{320,64},{384,128},{4... | collective-permute-start | bytes 393224 | tf_op jit(solution)/shard_map/ppermute | solution.py:29
  44.8 16.9 %collective-permute-start.3 = (bf16[4,64,512]{2,1,0:T(8,128)(2,1)S(1)}, bf16[4,64,512]{2,1,0:T(8,128)(2,1)S(1)}, u32[]{:S(2)}, u32[]{:S(2)}) collective-permute-start(bf16[4,64,512]{2,1,0:T(8,128)(2,1)S(1)} %pad_maximum_fusion.rest_0_), channel_id=1, source_target_pairs={{0,128},{64,448},{128,256},{192,64},{256,384},{320,192},{384,0},{4... | collective-permute-start | bytes 786440 | tf_op jit(solution)/shard_map/ppermute | solution.py:255
  51.9 13.3 %collective-permute-start.4 = (bf16[4,64,512]{2,1,0:T(8,128)(2,1)S(1)}, bf16[4,64,512]{2,1,0:T(8,128)(2,1)S(1)}, u32[]{:S(2)}, u32[]{:S(2)}) collective-permute-start(bf16[4,64,512]{2,1,0:T(8,128)(2,1)S(1)} %pad_maximum_fusion.rest_0_), channel_id=1, source_target_pairs={{0,448},{64,0},{128,64},{192,128},{256,192},{320,256},{384,320},{4... | collective-permute-start | bytes 786440 | tf_op jit(solution)/shard_map/ppermute | solution.py:255
  57.5 10.4 %collective-permute-start.5 = (bf16[4,64,512]{2,1,0:T(8,128)(2,1)S(1)}, bf16[4,64,512]{2,1,0:T(8,128)(2,1)S(1)}, u32[]{:S(2)}, u32[]{:S(2)}) collective-permute-start(bf16[4,64,512]{2,1,0:T(8,128)(2,1)S(1)} %pad_maximum_fusion.rest_0_), channel_id=1, source_target_pairs={{0,64},{64,128},{128,192},{192,256},{256,320},{320,384},{384,448},... | collective-permute-start | bytes 786440 | tf_op jit(solution)/shard_map/ppermute | solution.py:255
  69.8 42.5 %all-to-all-start.1 = ((bf16[64,64,128]{2,1,0:T(8,128)(2,1)}), bf16[64,64,128]{2,1,0:T(8,128)(2,1)S(1)}, u32[]{:S(2)}, u32[]{:S(2)}) async-start(bf16[64,64,128]{2,1,0:T(8,128)(2,1)} %project.1), calls=%async_computation.1 | async-start | bytes 2097152 | tf_op jit(solution)/shard_map/all_to_all | solution.py:24
  78.1 34.2 %copy-start.10 = (f32[72,128]{1,0:T(8,128)S(1)}, f32[72,128]{1,0:T(8,128)}, u32[]{:S(2)}) copy-start(f32[72,128]{1,0:T(8,128)} %constant.59.clone.refs_7_) | copy-start | bytes 110596
  78.1 34.2 %copy-start.11 = (f32[72,128]{1,0:T(8,128)S(1)}, f32[72,128]{1,0:T(8,128)}, u32[]{:S(2)}) copy-start(f32[72,128]{1,0:T(8,128)} %constant.60.clone.refs_8_) | copy-start | bytes 110596
  78.5 33.8 %copy-start.8 = (bf16[64,432]{1,0:T(8,128)(2,1)S(1)}, bf16[64,432]{1,0:T(8,128)(2,1)}, u32[]{:S(2)}) copy-start(bf16[64,432]{1,0:T(8,128)(2,1)} %constant.56.clone.refs_4_) | copy-start | bytes 165892
  78.5 33.8 %copy-start.9 = (bf16[144,128]{1,0:T(8,128)(2,1)S(1)}, bf16[144,128]{1,0:T(8,128)(2,1)}, u32[]{:S(2)}) copy-start(bf16[144,128]{1,0:T(8,128)(2,1)} %constant.55.clone.refs_3_) | copy-start | bytes 110596
  78.5 33.8 %copy-start.6 = (bf16[256,256]{1,0:T(8,128)(2,1)S(1)}, bf16[256,256]{1,0:T(8,128)(2,1)}, u32[]{:S(2)}) copy-start(bf16[256,256]{1,0:T(8,128)(2,1)} %constant.57.clone.refs_5_) | copy-start | bytes 393220
  78.5 33.8 %copy-start.7 = (bf16[256,256]{1,0:T(8,128)(2,1)S(1)}, bf16[256,256]{1,0:T(8,128)(2,1)}, u32[]{:S(2)}) copy-start(bf16[256,256]{1,0:T(8,128)(2,1)} %constant.58.clone.refs_6_) | copy-start | bytes 393220

commit v4 on v3

--- a/solution.py
+++ b/solution.py
@@ -203,11 +203,11 @@
     features = block_refs[0].shape[1]
     for shift, block_ref in zip(SHIFTS, block_refs):
         for e in range(4):
-            source = ((z - shift) & 7) ^ (4 * (e // 2))
+            source = ((z - shift) & 7) ^ (4 * (e % 2))
             if shift == 2:
                 source = source ^ (4 * (z & 1))
             place = (source & 6) + ((source & 1) ^ core)
-            at = pl.multiple_of((2 * place + (yh ^ (e % 2))) * features, features)
+            at = pl.multiple_of((2 * place + (yh ^ (e // 2))) * features, features)
             held_ref[pl.ds(at, features), :] = block_ref[e]
     weight = held_ref[...].T
     dests = out_ref.shape[0]
@@ -245,9 +245,9 @@
 
     count_z = SPLIT["z"]
     weight = out_weight.T
-    beside = flip(weight, "yh", 1)
+    beside = flip(weight, "z", 4)
     pair = jnp.stack([weight, beside])
-    opposite = flip(pair, "z", 4)
+    opposite = flip(pair, "yh", 1)
     blocks = [jnp.concatenate([pair, opposite])]
     for k in SHIFTS[1:]:
         turn = [(-k if k == 2 and i % 2 else k) for i in range(count_z)]
@@ -291,6 +291,7 @@
     padded = jnp.pad(taps[0], (0, tap_count + 1))
     toeplitz = jnp.tile(padded, tap_count)[: 2 * tap_count * tap_count]
     toeplitz = toeplitz.reshape(tap_count, 2 * tap_count)
+    back_taps = toeplitz[::-1, ::-1]
     first, last, high, low, cos_t, sin_t = spectral_tables()
     count = seq_devices * items
     scale = 1.0 / math.sqrt(row_count * seq_devices * per_group)
@@ -307,7 +308,7 @@
         cost_estimate=pl.CostEstimate(flops=1 << 31, bytes_accessed=4 << 20, transcendentals=0),
         compiler_params=pltpu.CompilerParams(vmem_limit_bytes=24 << 20),
         name="conv",
-    )(partial, toeplitz, toeplitz[::-1, ::-1], first, last, high, low, cos_t, sin_t)
+    )(partial, toeplitz, back_taps, first, last, high, low, cos_t, sin_t)
     home = home.reshape(seq_devices, 3 * items // 2, 2, row_count)[:, : items + 1]
     home = swap(home, SEQ)
     d_key = home[:, : items // 2].reshape(seq_devices, items, row_count)

time: 139 us -> 137 us (0.986)
  the two profiles are of different devices: /device:TPU:8 before, /device:TPU:9 now
where the time goes in v4:
time: 137 us; the launch traced here: 136 us
  starting transfers between devices  54 us (39%)
  waiting for transfers between devices  50.2 us (37%)
  blocking collectives  22.1 us (16%)
  Pallas kernels  5.52 us (4%)
  local copies, waits for them, and re-layouts  2.72 us (2%)
    all_to_all x2, waiting for transfers between devices, swap(): return lax.all_to_all(value, axes, split_axis=0, concat_axis=0, tiled=True)  33.8 us
    all_to_all x1, blocking collectives, swap(): return lax.all_to_all(value, axes, split_axis=0, concat_axis=0, tiled=True)  22.1 us
    ppermute x3, starting transfers between devices, flip(): return lax.ppermute(value, axis, [(i, i ^ bit) for i in range(count)])  21.8 us
    all_to_all x2, starting transfers between devices, swap(): return lax.all_to_all(value, axes, split_axis=0, concat_axis=0, tiled=True)  16.6 us
    ppermute x3, starting transfers between devices, local(): blocks.append(lax.ppermute(blocks[0], 'z', ring))  15.6 us
    ppermute x3, waiting for transfers between devices, flip(): return lax.ppermute(value, axis, [(i, i ^ bit) for i in range(count)])  8.7 us
    ppermute x3, waiting for transfers between devices, local(): blocks.append(lax.ppermute(blocks[0], 'z', ring))  7.76 us
    pallas_call x1, Pallas kernels, local(): pl.pallas_call(conv, out_shape=jax.ShapeDtypeStruct((seq_devices, 3 * ite...  2.8 us
  transfers between devices with their start and end apart: 8, of which 5 were waited for; matrix products, arithmetic and copies ran while one was open for 1% of the time, Pallas kernels for 0%

profile of v4, /device:TPU:9, one launch (start us, length us, event | category | flops | bytes accessed | tf_op | source)
XLA Modules:
  0.0 136.3 jit_solution(2202891013966995997)
XLA Ops:
  0.6 0.0 copy-start
  0.7 0.9 copy-done.1
  1.6 0.9 repeat.1
  2.4 7.4 %all-to-all-start = ((bf16[16,128,128]{2,1,0:T(8,128)(2,1)}), bf16[16,128,128]{2,1,0:T(8,128)(2,1)S(1)}, u32[]{:S(2)}, u32[]{:S(2)}) async-start(bf16[16,128,128]{2,1,0:T(8,128)(2,1)} %bitcast.1), calls=%async_computation | async-start | bytes 1048576 | tf_op jit(solution)/shard_map/all_to_all | solution.py:24
  9.8 10.6 %collective-permute-start.1 = (bf16[64,512]{1,0:T(8,128)(2,1)S(1)}, bf16[64,512]{1,0:T(8,128)(2,1)S(1)}, u32[]{:S(2)}, u32[]{:S(2)}) collective-permute-start(bf16[64,512]{1,0:T(8,128)(2,1)S(1)} %bitcast.31), channel_id=1, source_target_pairs={{0,256},{64,320},{128,384},{192,448},{256,0},{320,64},{384,128},{4... | collective-permute-start | bytes 196616 | tf_op jit(solution)/shard_map/ppermute | solution.py:29
  20.5 0.6 all-to-all-done
  21.0 6.3 %collective-permute-start = (bf16[16,128,128]{2,1,0:T(8,128)(2,1)S(1)}, bf16[16,128,128]{2,1,0:T(8,128)(2,1)S(1)}, u32[]{:S(2)}, u32[]{:S(2)}) collective-permute-start(bf16[16,128,128]{2,1,0:T(8,128)(2,1)S(1)} %all-to-all-done), channel_id=1, source_target_pairs={{0,1},{1,0},{2,3},{3,2},{4,5},{5,4},{6,7},{7,6},{8,9},{9,8},{10,11... | collective-permute-start | bytes 1572872 | tf_op jit(solution)/shard_map/ppermute | solution.py:29
  27.4 0.0 copy-start.2
  27.4 0.0 copy-start.5
  27.4 4.8 %collective-permute-start.2 = (bf16[2,64,512]{2,1,0:T(8,128)(2,1)S(1)}, bf16[2,64,512]{2,1,0:T(8,128)(2,1)S(1)}, u32[]{:S(2)}, u32[]{:S(2)}) collective-permute-start(bf16[2,64,512]{2,1,0:T(8,128)(2,1)S(1)} %pad_maximum_fusion.1), channel_id=1, source_target_pairs={{0,8},{8,0},{1,9},{9,1},{2,10},{10,2},{3,11},{11,3},{4,12},{12,4},... | collective-permute-start | bytes 393224 | tf_op jit(solution)/shard_map/ppermute | solution.py:29
  32.2 8.7 %collective-permute-done.2 = bf16[2,64,512]{2,1,0:T(8,128)(2,1)S(1)} collective-permute-done((bf16[2,64,512]{2,1,0:T(8,128)(2,1)S(1)}, bf16[2,64,512]{2,1,0:T(8,128)(2,1)S(1)}, u32[]{:S(2)}, u32[]{:S(2)}) %collective-permute-start.2) | collective-permute-done | bytes 131104 | tf_op jit(solution)/shard_map/ppermute | solution.py:29
  41.0 5.8 %collective-permute-start.3 = (bf16[4,64,512]{2,1,0:T(8,128)(2,1)S(1)}, bf16[4,64,512]{2,1,0:T(8,128)(2,1)S(1)}, u32[]{:S(2)}, u32[]{:S(2)}) collective-permute-start(bf16[4,64,512]{2,1,0:T(8,128)(2,1)S(1)} %pad_maximum_fusion.rest_0_), channel_id=1, source_target_pairs={{0,128},{64,448},{128,256},{192,64},{256,384},{320,192},{384,0},{4... | collective-permute-start | bytes 786440 | tf_op jit(solution)/shard_map/ppermute | solution.py:255
  46.7 7.0 %collective-permute-start.4 = (bf16[4,64,512]{2,1,0:T(8,128)(2,1)S(1)}, bf16[4,64,512]{2,1,0:T(8,128)(2,1)S(1)}, u32[]{:S(2)}, u32[]{:S(2)}) collective-permute-start(bf16[4,64,512]{2,1,0:T(8,128)(2,1)S(1)} %pad_maximum_fusion.rest_0_), channel_id=1, source_target_pairs={{0,448},{64,0},{128,64},{192,128},{256,192},{320,256},{384,320},{4... | collective-permute-start | bytes 786440 | tf_op jit(solution)/shard_map/ppermute | solution.py:255
  53.8 2.8 %collective-permute-start.5 = (bf16[4,64,512]{2,1,0:T(8,128)(2,1)S(1)}, bf16[4,64,512]{2,1,0:T(8,128)(2,1)S(1)}, u32[]{:S(2)}, u32[]{:S(2)}) collective-permute-start(bf16[4,64,512]{2,1,0:T(8,128)(2,1)S(1)} %pad_maximum_fusion.rest_0_), channel_id=1, source_target_pairs={{0,64},{64,128},{128,192},{192,256},{256,320},{320,384},{384,448},... | collective-permute-start | bytes 786440 | tf_op jit(solution)/shard_map/ppermute | solution.py:255
  56.6 1.2 collective-permute-done.3.rest_1_
  57.8 6.6 %collective-permute-done.4.rest_2_ = bf16[4,64,512]{2,1,0:T(8,128)(2,1)S(1)} collective-permute-done((bf16[4,64,512]{2,1,0:T(8,128)(2,1)S(1)}, bf16[4,64,512]{2,1,0:T(8,128)(2,1)S(1)}, u32[]{:S(2)}, u32[]{:S(2)}) %collective-permute-start.4) | collective-permute-done | bytes 262176 | tf_op jit(solution)/shard_map/ppermute | solution.py:255
  64.4 1.8 %project.1 = bf16[64,64,128]{2,1,0:T(8,128)(2,1)} custom-call(bf16[4,4,128,128]{3,2,1,0:T(8,128)(2,1)S(1)} %bitcast.23, bf16[4,4,128,128]{3,2,1,0:T(8,128)(2,1)S(1)} %bitcast.24, bf16[4,64,512]{2,1,0:T(8,128)(2,1)S(1)} %pad_maximum_fusion.rest_0_, bf16[4,64,512]{2,1,0:T(8,128)(2,1)S(1)} %collective-permute-done.3.rest_1_, ...), custom_call_target="tpu_custom_call" | custom-call | flops 536870912 | bytes 3145728 | tf_op jit(solution)/shard_map/project/pallas_call | solution.py:273
  66.3 9.3 %all-to-all-start.1 = ((bf16[64,64,128]{2,1,0:T(8,128)(2,1)}), bf16[64,64,128]{2,1,0:T(8,128)(2,1)S(1)}, u32[]{:S(2)}, u32[]{:S(2)}) async-start(bf16[64,64,128]{2,1,0:T(8,128)(2,1)} %project.1), calls=%async_computation.1 | async-start | bytes 2097152 | tf_op jit(solution)/shard_map/all_to_all | solution.py:24
  75.6 0.0 copy-start.10
  75.6 0.0 copy-start.11
  75.6 0.3 tile.10
  76.0 0.0 copy-start.8
  76.0 0.0 copy-start.9
  76.0 0.0 copy-start.6
  76.0 0.0 copy-start.7
  76.1 0.2 rev.3.refs_2_
  76.3 33.2 %all-to-all-done.1.refs_0_ = bf16[64,64,128]{2,1,0:T(8,128)(2,1)S(1)} async-done(((bf16[64,64,128]{2,1,0:T(8,128)(2,1)}), bf16[64,64,128]{2,1,0:T(8,128)(2,1)S(1)}, u32[]{:S(2)}, u32[]{:S(2)}) %all-to-all-start.1) | async-done | bytes 1048608 | tf_op jit(solution)/shard_map/all_to_all | solution.py:24
  109.5 2.8 %conv.1 = bf16[64,24,128]{2,1,0:T(8,128)(2,1)S(1)} custom-call(bf16[64,64,128]{2,1,0:T(8,128)(2,1)S(1)} %all-to-all-done.1.refs_0_, bf16[128,256]{1,0:T(8,128)(2,1)S(1)} %reshape.51.refs_1_, bf16[128,256]{1,0:T(8,128)(2,1)S(1)} %rev.3.refs_2_, bf16[144,128]{1,0:T(8,128)(2,1)S(1)} %copy-done.9, bf16[64,432]{1,0:T(8,128)(2,1)S(1)} %copy-done.8, ...), custom_call_target="tpu_custom_call" | custom-call | flops 2147483648 | bytes 4194304 | tf_op jit(solution)/shard_map/conv/pallas_call | solution.py:302
  112.4 0.2 slice.29
  112.6 22.1 %all_to_all.15 = bf16[64,9,2,128]{3,2,1,0:T(2,128)(2,1)S(1)} all-to-all(bf16[64,9,2,128]{3,2,1,0:T(2,128)(2,1)S(1)} %slice.29), channel_id=1, replica_groups=mesh['z'=8,'x'=4,'yh'=2,'yl'=4,'core'=2] {'z','x','yh'}, dimensions={0} | all-to-all | bytes 589824 | tf_op jit(solution)/shard_map/all_to_all | solution.py:24
  134.8 0.6 reduce_sum.9
  135.4 0.9 fusion.1
  (28 shorter events, 0.2 us)
Async XLA Ops:
  0.6 74.9 %copy-start = (bf16[32,128]{1,0:T(8,128)(2,1)S(1)}, bf16[32,128]{1,0:T(8,128)(2,1)}, u32[]{:S(2)}) copy-start(bf16[32,128]{1,0:T(8,128)(2,1)} %param.19) | copy-start | bytes 24580
  0.6 0.9 copy-start.1
  2.4 7.4 %copy-start.12 = (bf16[512,64]{0,1:T(8,128)(2,1)S(1)}, bf16[512,64]{0,1:T(8,128)(2,1)}, u32[]{:S(2)}) copy-start(bf16[512,64]{0,1:T(8,128)(2,1)} %param.17) | copy-start | bytes 196612
  2.4 18.6 %all-to-all-start = ((bf16[16,128,128]{2,1,0:T(8,128)(2,1)}), bf16[16,128,128]{2,1,0:T(8,128)(2,1)S(1)}, u32[]{:S(2)}, u32[]{:S(2)}) async-start(bf16[16,128,128]{2,1,0:T(8,128)(2,1)} %bitcast.1), calls=%async_computation | async-start | bytes 1048576 | tf_op jit(solution)/shard_map/all_to_all | solution.py:24
  9.8 17.5 %collective-permute-start.1 = (bf16[64,512]{1,0:T(8,128)(2,1)S(1)}, bf16[64,512]{1,0:T(8,128)(2,1)S(1)}, u32[]{:S(2)}, u32[]{:S(2)}) collective-permute-start(bf16[64,512]{1,0:T(8,128)(2,1)S(1)} %bitcast.31), channel_id=1, source_target_pairs={{0,256},{64,320},{128,384},{192,448},{256,0},{320,64},{384,128},{4... | collective-permute-start | bytes 196616 | tf_op jit(solution)/shard_map/ppermute | solution.py:29
  21.0 43.4 %collective-permute-start = (bf16[16,128,128]{2,1,0:T(8,128)(2,1)S(1)}, bf16[16,128,128]{2,1,0:T(8,128)(2,1)S(1)}, u32[]{:S(2)}, u32[]{:S(2)}) collective-permute-start(bf16[16,128,128]{2,1,0:T(8,128)(2,1)S(1)} %all-to-all-done), channel_id=1, source_target_pairs={{0,1},{1,0},{2,3},{3,2},{4,5},{5,4},{6,7},{7,6},{8,9},{9,8},{10,11... | collective-permute-start | bytes 1572872 | tf_op jit(solution)/shard_map/ppermute | solution.py:29
  27.4 37.0 %copy-start.2 = (bf16[512,128]{1,0:T(8,128)(2,1)S(1)}, bf16[512,128]{1,0:T(8,128)(2,1)}, u32[]{:S(2)}) copy-start(bf16[512,128]{1,0:T(8,128)(2,1)} %param.18) | copy-start | bytes 393220
  27.4 37.0 %copy-start.3 = (bf16[512,128]{1,0:T(8,128)(2,1)S(1)}, bf16[512,128]{1,0:T(8,128)(2,1)}, u32[]{:S(2)}) copy-start(bf16[512,128]{1,0:T(8,128)(2,1)} %param.14) | copy-start | bytes 393220
  27.4 37.0 %copy-start.4 = (bf16[512,128]{1,0:T(8,128)(2,1)S(1)}, bf16[512,128]{1,0:T(8,128)(2,1)}, u32[]{:S(2)}) copy-start(bf16[512,128]{1,0:T(8,128)(2,1)} %param.15) | copy-start | bytes 393220
  27.4 37.0 %copy-start.5 = (bf16[512,128]{1,0:T(8,128)(2,1)S(1)}, bf16[512,128]{1,0:T(8,128)(2,1)}, u32[]{:S(2)}) copy-start(bf16[512,128]{1,0:T(8,128)(2,1)} %param.13) | copy-start | bytes 393220
  27.4 13.5 %collective-permute-start.2 = (bf16[2,64,512]{2,1,0:T(8,128)(2,1)S(1)}, bf16[2,64,512]{2,1,0:T(8,128)(2,1)S(1)}, u32[]{:S(2)}, u32[]{:S(2)}) collective-permute-start(bf16[2,64,512]{2,1,0:T(8,128)(2,1)S(1)} %pad_maximum_fusion.1), channel_id=1, source_target_pairs={{0,8},{8,0},{1,9},{9,1},{2,10},{10,2},{3,11},{11,3},{4,12},{12,4},... | collective-permute-start | bytes 393224 | tf_op jit(solution)/shard_map/ppermute | solution.py:29
  41.0 16.8 %collective-permute-start.3 = (bf16[4,64,512]{2,1,0:T(8,128)(2,1)S(1)}, bf16[4,64,512]{2,1,0:T(8,128)(2,1)S(1)}, u32[]{:S(2)}, u32[]{:S(2)}) collective-permute-start(bf16[4,64,512]{2,1,0:T(8,128)(2,1)S(1)} %pad_maximum_fusion.rest_0_), channel_id=1, source_target_pairs={{0,128},{64,448},{128,256},{192,64},{256,384},{320,192},{384,0},{4... | collective-permute-start | bytes 786440 | tf_op jit(solution)/shard_map/ppermute | solution.py:255
  46.7 17.6 %collective-permute-start.4 = (bf16[4,64,512]{2,1,0:T(8,128)(2,1)S(1)}, bf16[4,64,512]{2,1,0:T(8,128)(2,1)S(1)}, u32[]{:S(2)}, u32[]{:S(2)}) collective-permute-start(bf16[4,64,512]{2,1,0:T(8,128)(2,1)S(1)} %pad_maximum_fusion.rest_0_), channel_id=1, source_target_pairs={{0,448},{64,0},{128,64},{192,128},{256,192},{320,256},{384,320},{4... | collective-permute-start | bytes 786440 | tf_op jit(solution)/shard_map/ppermute | solution.py:255
  53.8 10.6 %collective-permute-start.5 = (bf16[4,64,512]{2,1,0:T(8,128)(2,1)S(1)}, bf16[4,64,512]{2,1,0:T(8,128)(2,1)S(1)}, u32[]{:S(2)}, u32[]{:S(2)}) collective-permute-start(bf16[4,64,512]{2,1,0:T(8,128)(2,1)S(1)} %pad_maximum_fusion.rest_0_), channel_id=1, source_target_pairs={{0,64},{64,128},{128,192},{192,256},{256,320},{320,384},{384,448},... | collective-permute-start | bytes 786440 | tf_op jit(solution)/shard_map/ppermute | solution.py:255
  66.3 43.2 %all-to-all-start.1 = ((bf16[64,64,128]{2,1,0:T(8,128)(2,1)}), bf16[64,64,128]{2,1,0:T(8,128)(2,1)S(1)}, u32[]{:S(2)}, u32[]{:S(2)}) async-start(bf16[64,64,128]{2,1,0:T(8,128)(2,1)} %project.1), calls=%async_computation.1 | async-start | bytes 2097152 | tf_op jit(solution)/shard_map/all_to_all | solution.py:24
  75.6 33.9 %copy-start.10 = (f32[72,128]{1,0:T(8,128)S(1)}, f32[72,128]{1,0:T(8,128)}, u32[]{:S(2)}) copy-start(f32[72,128]{1,0:T(8,128)} %constant.59.clone.refs_7_) | copy-start | bytes 110596
  75.6 33.9 %copy-start.11 = (f32[72,128]{1,0:T(8,128)S(1)}, f32[72,128]{1,0:T(8,128)}, u32[]{:S(2)}) copy-start(f32[72,128]{1,0:T(8,128)} %constant.60.clone.refs_8_) | copy-start | bytes 110596
  76.0 33.5 %copy-start.8 = (bf16[64,432]{1,0:T(8,128)(2,1)S(1)}, bf16[64,432]{1,0:T(8,128)(2,1)}, u32[]{:S(2)}) copy-start(bf16[64,432]{1,0:T(8,128)(2,1)} %constant.56.clone.refs_4_) | copy-start | bytes 165892
  76.0 33.5 %copy-start.9 = (bf16[144,128]{1,0:T(8,128)(2,1)S(1)}, bf16[144,128]{1,0:T(8,128)(2,1)}, u32[]{:S(2)}) copy-start(bf16[144,128]{1,0:T(8,128)(2,1)} %constant.55.clone.refs_3_) | copy-start | bytes 110596
  76.0 33.5 %copy-start.6 = (bf16[256,256]{1,0:T(8,128)(2,1)S(1)}, bf16[256,256]{1,0:T(8,128)(2,1)}, u32[]{:S(2)}) copy-start(bf16[256,256]{1,0:T(8,128)(2,1)} %constant.57.clone.refs_5_) | copy-start | bytes 393220
  76.0 33.5 %copy-start.7 = (bf16[256,256]{1,0:T(8,128)(2,1)S(1)}, bf16[256,256]{1,0:T(8,128)(2,1)}, u32[]{:S(2)}) copy-start(bf16[256,256]{1,0:T(8,128)(2,1)} %constant.58.clone.refs_6_) | copy-start | bytes 393220

commit v5 on v4

--- a/solution.py
+++ b/solution.py
@@ -234,6 +234,14 @@
         out_ref[:, y] = grad_ref[...]
 
 
+def unpack_kernel(home_ref, key_ref, value_ref, filter_ref):
+    half = key_ref.shape[1]
+    key_ref[...] = home_ref[:, :half]
+    value_ref[...] = home_ref[:, half : 2 * half]
+    both = home_ref[:, 2 * half].astype(jnp.float32).reshape(filter_ref.shape[0], -1, filter_ref.shape[1])
+    filter_ref[...] = jnp.sum(both, axis=1)
+
+
 def local(queries, key_feat, value_feat, out_grad, out_weight, long_filter, short_filter):
     channels, row_count = out_grad.shape
     group_count, tap_count = short_filter.shape
@@ -311,11 +319,19 @@
     )(partial, toeplitz, back_taps, first, last, high, low, cos_t, sin_t)
     home = home.reshape(seq_devices, 3 * items // 2, 2, row_count)[:, : items + 1]
     home = swap(home, SEQ)
-    d_key = home[:, : items // 2].reshape(seq_devices, items, row_count)
-    d_value = home[:, items // 2 : items].reshape(seq_devices, items, row_count)
-    both = home[:, items].astype(jnp.float32)
-    both = both[:, 0] + both[:, 1]
-    d_filter = jnp.sum(both.reshape(group_count, seq_devices // group_count, tap_count), axis=1)
+    pairs = (seq_devices, items // 2, 2, row_count)
+    d_key, d_value, d_filter = pl.pallas_call(
+        unpack_kernel,
+        out_shape=(
+            jax.ShapeDtypeStruct(pairs, jnp.bfloat16),
+            jax.ShapeDtypeStruct(pairs, jnp.bfloat16),
+            jax.ShapeDtypeStruct((group_count, tap_count), jnp.float32),
+        ),
+        in_specs=[VMEM],
+        out_specs=(VMEM,) * 3,
+        compiler_params=pltpu.CompilerParams(vmem_limit_bytes=4 << 20),
+        name="unpack",
+    )(home)
     return (d_key.reshape(channels, row_count), d_value.reshape(channels, row_count), d_filter)
 
 

time: 137 us -> 136 us (level)
  no operation moved by 1% of the time
where the time goes in v5:
time: 136 us; the launch traced here: 135 us
  starting transfers between devices  54 us (40%)
  waiting for transfers between devices  50.2 us (37%)
  blocking collectives  22.1 us (16%)
  Pallas kernels  6.28 us (5%)
  local copies, waits for them, and re-layouts  1.84 us (1%)
    all_to_all x2, waiting for transfers between devices, swap(): return lax.all_to_all(value, axes, split_axis=0, concat_axis=0, tiled=True)  33.8 us
    all_to_all x1, blocking collectives, swap(): return lax.all_to_all(value, axes, split_axis=0, concat_axis=0, tiled=True)  22.1 us
    ppermute x3, starting transfers between devices, flip(): return lax.ppermute(value, axis, [(i, i ^ bit) for i in range(count)])  21.8 us
    all_to_all x2, starting transfers between devices, swap(): return lax.all_to_all(value, axes, split_axis=0, concat_axis=0, tiled=True)  16.6 us
    ppermute x3, starting transfers between devices, local(): blocks.append(lax.ppermute(blocks[0], 'z', ring))  15.6 us
    ppermute x3, waiting for transfers between devices, flip(): return lax.ppermute(value, axis, [(i, i ^ bit) for i in range(count)])  8.7 us
    ppermute x3, waiting for transfers between devices, local(): blocks.append(lax.ppermute(blocks[0], 'z', ring))  7.76 us
    pallas_call x1, Pallas kernels, local(): pl.pallas_call(conv, out_shape=jax.ShapeDtypeStruct((seq_devices, 3 * ite...  2.8 us
  transfers between devices with their start and end apart: 8, of which 5 were waited for; matrix products, arithmetic and copies ran while one was open for 1% of the time, Pallas kernels for 0%

profile of v5, /device:TPU:9, one launch (start us, length us, event | category | flops | bytes accessed | tf_op | source)
XLA Modules:
  0.0 135.5 jit_solution(7275612685585692368)
XLA Ops:
  0.6 0.0 copy-start
  0.7 0.9 copy-done.1
  1.6 0.9 repeat.1
  2.4 7.4 %all-to-all-start = ((bf16[16,128,128]{2,1,0:T(8,128)(2,1)}), bf16[16,128,128]{2,1,0:T(8,128)(2,1)S(1)}, u32[]{:S(2)}, u32[]{:S(2)}) async-start(bf16[16,128,128]{2,1,0:T(8,128)(2,1)} %bitcast.1), calls=%async_computation | async-start | bytes 1048576 | tf_op jit(solution)/shard_map/all_to_all | solution.py:24
  9.8 10.6 %collective-permute-start.1 = (bf16[64,512]{1,0:T(8,128)(2,1)S(1)}, bf16[64,512]{1,0:T(8,128)(2,1)S(1)}, u32[]{:S(2)}, u32[]{:S(2)}) collective-permute-start(bf16[64,512]{1,0:T(8,128)(2,1)S(1)} %bitcast.25), channel_id=1, source_target_pairs={{0,256},{64,320},{128,384},{192,448},{256,0},{320,64},{384,128},{4... | collective-permute-start | bytes 196616 | tf_op jit(solution)/shard_map/ppermute | solution.py:29
  20.4 0.6 all-to-all-done
  21.0 6.3 %collective-permute-start = (bf16[16,128,128]{2,1,0:T(8,128)(2,1)S(1)}, bf16[16,128,128]{2,1,0:T(8,128)(2,1)S(1)}, u32[]{:S(2)}, u32[]{:S(2)}) collective-permute-start(bf16[16,128,128]{2,1,0:T(8,128)(2,1)S(1)} %all-to-all-done), channel_id=1, source_target_pairs={{0,1},{1,0},{2,3},{3,2},{4,5},{5,4},{6,7},{7,6},{8,9},{9,8},{10,11... | collective-permute-start | bytes 1572872 | tf_op jit(solution)/shard_map/ppermute | solution.py:29
  27.4 0.0 copy-start.2
  27.4 0.0 copy-start.3
  27.4 0.0 copy-start.5
  27.4 4.8 %collective-permute-start.2 = (bf16[2,64,512]{2,1,0:T(8,128)(2,1)S(1)}, bf16[2,64,512]{2,1,0:T(8,128)(2,1)S(1)}, u32[]{:S(2)}, u32[]{:S(2)}) collective-permute-start(bf16[2,64,512]{2,1,0:T(8,128)(2,1)S(1)} %pad_maximum_fusion.1), channel_id=1, source_target_pairs={{0,8},{8,0},{1,9},{9,1},{2,10},{10,2},{3,11},{11,3},{4,12},{12,4},... | collective-permute-start | bytes 393224 | tf_op jit(solution)/shard_map/ppermute | solution.py:29
  32.2 8.7 %collective-permute-done.2 = bf16[2,64,512]{2,1,0:T(8,128)(2,1)S(1)} collective-permute-done((bf16[2,64,512]{2,1,0:T(8,128)(2,1)S(1)}, bf16[2,64,512]{2,1,0:T(8,128)(2,1)S(1)}, u32[]{:S(2)}, u32[]{:S(2)}) %collective-permute-start.2) | collective-permute-done | bytes 131104 | tf_op jit(solution)/shard_map/ppermute | solution.py:29
  41.0 5.8 %collective-permute-start.3 = (bf16[4,64,512]{2,1,0:T(8,128)(2,1)S(1)}, bf16[4,64,512]{2,1,0:T(8,128)(2,1)S(1)}, u32[]{:S(2)}, u32[]{:S(2)}) collective-permute-start(bf16[4,64,512]{2,1,0:T(8,128)(2,1)S(1)} %pad_maximum_fusion.rest_0_), channel_id=1, source_target_pairs={{0,128},{64,448},{128,256},{192,64},{256,384},{320,192},{384,0},{4... | collective-permute-start | bytes 786440 | tf_op jit(solution)/shard_map/ppermute | solution.py:263
  46.7 7.0 %collective-permute-start.4 = (bf16[4,64,512]{2,1,0:T(8,128)(2,1)S(1)}, bf16[4,64,512]{2,1,0:T(8,128)(2,1)S(1)}, u32[]{:S(2)}, u32[]{:S(2)}) collective-permute-start(bf16[4,64,512]{2,1,0:T(8,128)(2,1)S(1)} %pad_maximum_fusion.rest_0_), channel_id=1, source_target_pairs={{0,448},{64,0},{128,64},{192,128},{256,192},{320,256},{384,320},{4... | collective-permute-start | bytes 786440 | tf_op jit(solution)/shard_map/ppermute | solution.py:263
  53.8 2.8 %collective-permute-start.5 = (bf16[4,64,512]{2,1,0:T(8,128)(2,1)S(1)}, bf16[4,64,512]{2,1,0:T(8,128)(2,1)S(1)}, u32[]{:S(2)}, u32[]{:S(2)}) collective-permute-start(bf16[4,64,512]{2,1,0:T(8,128)(2,1)S(1)} %pad_maximum_fusion.rest_0_), channel_id=1, source_target_pairs={{0,64},{64,128},{128,192},{192,256},{256,320},{320,384},{384,448},... | collective-permute-start | bytes 786440 | tf_op jit(solution)/shard_map/ppermute | solution.py:263
  56.6 1.2 collective-permute-done.3.rest_1_
  57.8 6.6 %collective-permute-done.4.rest_2_ = bf16[4,64,512]{2,1,0:T(8,128)(2,1)S(1)} collective-permute-done((bf16[4,64,512]{2,1,0:T(8,128)(2,1)S(1)}, bf16[4,64,512]{2,1,0:T(8,128)(2,1)S(1)}, u32[]{:S(2)}, u32[]{:S(2)}) %collective-permute-start.4) | collective-permute-done | bytes 262176 | tf_op jit(solution)/shard_map/ppermute | solution.py:263
  64.4 1.8 %project.1 = bf16[64,64,128]{2,1,0:T(8,128)(2,1)} custom-call(bf16[4,4,128,128]{3,2,1,0:T(8,128)(2,1)S(1)} %bitcast.17, bf16[4,4,128,128]{3,2,1,0:T(8,128)(2,1)S(1)} %bitcast.18, bf16[4,64,512]{2,1,0:T(8,128)(2,1)S(1)} %pad_maximum_fusion.rest_0_, bf16[4,64,512]{2,1,0:T(8,128)(2,1)S(1)} %collective-permute-done.3.rest_1_, ...), custom_call_target="tpu_custom_call" | custom-call | flops 536870912 | bytes 3145728 | tf_op jit(solution)/shard_map/project/pallas_call | solution.py:281
  66.3 9.3 %all-to-all-start.1 = ((bf16[64,64,128]{2,1,0:T(8,128)(2,1)}), bf16[64,64,128]{2,1,0:T(8,128)(2,1)S(1)}, u32[]{:S(2)}, u32[]{:S(2)}) async-start(bf16[64,64,128]{2,1,0:T(8,128)(2,1)} %project.1), calls=%async_computation.1 | async-start | bytes 2097152 | tf_op jit(solution)/shard_map/all_to_all | solution.py:24
  75.6 0.0 copy-start.10
  75.6 0.0 copy-start.11
  75.6 0.3 tile.10
  76.0 0.0 copy-start.8
  76.0 0.0 copy-start.9
  76.0 0.0 copy-start.6
  76.0 0.0 copy-start.7
  76.1 0.2 rev.3.refs_2_
  76.3 33.2 %all-to-all-done.1.refs_0_ = bf16[64,64,128]{2,1,0:T(8,128)(2,1)S(1)} async-done(((bf16[64,64,128]{2,1,0:T(8,128)(2,1)}), bf16[64,64,128]{2,1,0:T(8,128)(2,1)S(1)}, u32[]{:S(2)}, u32[]{:S(2)}) %all-to-all-start.1) | async-done | bytes 1048608 | tf_op jit(solution)/shard_map/all_to_all | solution.py:24
  109.6 2.8 %conv.1 = bf16[64,24,128]{2,1,0:T(8,128)(2,1)S(1)} custom-call(bf16[64,64,128]{2,1,0:T(8,128)(2,1)S(1)} %all-to-all-done.1.refs_0_, bf16[128,256]{1,0:T(8,128)(2,1)S(1)} %reshape.51.refs_1_, bf16[128,256]{1,0:T(8,128)(2,1)S(1)} %rev.3.refs_2_, bf16[144,128]{1,0:T(8,128)(2,1)S(1)} %copy-done.9, bf16[64,432]{1,0:T(8,128)(2,1)S(1)} %copy-done.8, ...), custom_call_target="tpu_custom_call" | custom-call | flops 2147483648 | bytes 4194304 | tf_op jit(solution)/shard_map/conv/pallas_call | solution.py:310
  112.4 0.2 slice.9
  112.6 22.1 %all_to_all.15.home_ref = bf16[64,9,2,128]{3,2,1,0:T(2,128)(2,1)S(1)} all-to-all(bf16[64,9,2,128]{3,2,1,0:T(2,128)(2,1)S(1)} %slice.9), channel_id=1, replica_groups=mesh['z'=8,'x'=4,'yh'=2,'yl'=4,'core'=2] {'z','x','yh'}, dimensions={0} | all-to-all | bytes 589824 | tf_op jit(solution)/shard_map/all_to_all | solution.py:24
  134.7 0.8 unpack.1
  (25 shorter events, 0.1 us)
Async XLA Ops:
  0.6 74.9 %copy-start = (bf16[32,128]{1,0:T(8,128)(2,1)S(1)}, bf16[32,128]{1,0:T(8,128)(2,1)}, u32[]{:S(2)}) copy-start(bf16[32,128]{1,0:T(8,128)(2,1)} %param.19) | copy-start | bytes 24580
  0.6 0.9 copy-start.1
  2.4 7.4 %copy-start.12 = (bf16[512,64]{0,1:T(8,128)(2,1)S(1)}, bf16[512,64]{0,1:T(8,128)(2,1)}, u32[]{:S(2)}) copy-start(bf16[512,64]{0,1:T(8,128)(2,1)} %param.17) | copy-start | bytes 196612
  2.4 18.6 %all-to-all-start = ((bf16[16,128,128]{2,1,0:T(8,128)(2,1)}), bf16[16,128,128]{2,1,0:T(8,128)(2,1)S(1)}, u32[]{:S(2)}, u32[]{:S(2)}) async-start(bf16[16,128,128]{2,1,0:T(8,128)(2,1)} %bitcast.1), calls=%async_computation | async-start | bytes 1048576 | tf_op jit(solution)/shard_map/all_to_all | solution.py:24
  9.8 17.5 %collective-permute-start.1 = (bf16[64,512]{1,0:T(8,128)(2,1)S(1)}, bf16[64,512]{1,0:T(8,128)(2,1)S(1)}, u32[]{:S(2)}, u32[]{:S(2)}) collective-permute-start(bf16[64,512]{1,0:T(8,128)(2,1)S(1)} %bitcast.25), channel_id=1, source_target_pairs={{0,256},{64,320},{128,384},{192,448},{256,0},{320,64},{384,128},{4... | collective-permute-start | bytes 196616 | tf_op jit(solution)/shard_map/ppermute | solution.py:29
  21.0 43.4 %collective-permute-start = (bf16[16,128,128]{2,1,0:T(8,128)(2,1)S(1)}, bf16[16,128,128]{2,1,0:T(8,128)(2,1)S(1)}, u32[]{:S(2)}, u32[]{:S(2)}) collective-permute-start(bf16[16,128,128]{2,1,0:T(8,128)(2,1)S(1)} %all-to-all-done), channel_id=1, source_target_pairs={{0,1},{1,0},{2,3},{3,2},{4,5},{5,4},{6,7},{7,6},{8,9},{9,8},{10,11... | collective-permute-start | bytes 1572872 | tf_op jit(solution)/shard_map/ppermute | solution.py:29
  27.4 37.0 %copy-start.2 = (bf16[512,128]{1,0:T(8,128)(2,1)S(1)}, bf16[512,128]{1,0:T(8,128)(2,1)}, u32[]{:S(2)}) copy-start(bf16[512,128]{1,0:T(8,128)(2,1)} %param.18) | copy-start | bytes 393220
  27.4 37.0 %copy-start.3 = (bf16[512,128]{1,0:T(8,128)(2,1)S(1)}, bf16[512,128]{1,0:T(8,128)(2,1)}, u32[]{:S(2)}) copy-start(bf16[512,128]{1,0:T(8,128)(2,1)} %param.14) | copy-start | bytes 393220
  27.4 37.0 %copy-start.4 = (bf16[512,128]{1,0:T(8,128)(2,1)S(1)}, bf16[512,128]{1,0:T(8,128)(2,1)}, u32[]{:S(2)}) copy-start(bf16[512,128]{1,0:T(8,128)(2,1)} %param.15) | copy-start | bytes 393220
  27.4 37.0 %copy-start.5 = (bf16[512,128]{1,0:T(8,128)(2,1)S(1)}, bf16[512,128]{1,0:T(8,128)(2,1)}, u32[]{:S(2)}) copy-start(bf16[512,128]{1,0:T(8,128)(2,1)} %param.13) | copy-start | bytes 393220
  27.4 13.5 %collective-permute-start.2 = (bf16[2,64,512]{2,1,0:T(8,128)(2,1)S(1)}, bf16[2,64,512]{2,1,0:T(8,128)(2,1)S(1)}, u32[]{:S(2)}, u32[]{:S(2)}) collective-permute-start(bf16[2,64,512]{2,1,0:T(8,128)(2,1)S(1)} %pad_maximum_fusion.1), channel_id=1, source_target_pairs={{0,8},{8,0},{1,9},{9,1},{2,10},{10,2},{3,11},{11,3},{4,12},{12,4},... | collective-permute-start | bytes 393224 | tf_op jit(solution)/shard_map/ppermute | solution.py:29
  41.0 16.8 %collective-permute-start.3 = (bf16[4,64,512]{2,1,0:T(8,128)(2,1)S(1)}, bf16[4,64,512]{2,1,0:T(8,128)(2,1)S(1)}, u32[]{:S(2)}, u32[]{:S(2)}) collective-permute-start(bf16[4,64,512]{2,1,0:T(8,128)(2,1)S(1)} %pad_maximum_fusion.rest_0_), channel_id=1, source_target_pairs={{0,128},{64,448},{128,256},{192,64},{256,384},{320,192},{384,0},{4... | collective-permute-start | bytes 786440 | tf_op jit(solution)/shard_map/ppermute | solution.py:263
  46.7 17.6 %collective-permute-start.4 = (bf16[4,64,512]{2,1,0:T(8,128)(2,1)S(1)}, bf16[4,64,512]{2,1,0:T(8,128)(2,1)S(1)}, u32[]{:S(2)}, u32[]{:S(2)}) collective-permute-start(bf16[4,64,512]{2,1,0:T(8,128)(2,1)S(1)} %pad_maximum_fusion.rest_0_), channel_id=1, source_target_pairs={{0,448},{64,0},{128,64},{192,128},{256,192},{320,256},{384,320},{4... | collective-permute-start | bytes 786440 | tf_op jit(solution)/shard_map/ppermute | solution.py:263
  53.8 10.6 %collective-permute-start.5 = (bf16[4,64,512]{2,1,0:T(8,128)(2,1)S(1)}, bf16[4,64,512]{2,1,0:T(8,128)(2,1)S(1)}, u32[]{:S(2)}, u32[]{:S(2)}) collective-permute-start(bf16[4,64,512]{2,1,0:T(8,128)(2,1)S(1)} %pad_maximum_fusion.rest_0_), channel_id=1, source_target_pairs={{0,64},{64,128},{128,192},{192,256},{256,320},{320,384},{384,448},... | collective-permute-start | bytes 786440 | tf_op jit(solution)/shard_map/ppermute | solution.py:263
  66.3 43.2 %all-to-all-start.1 = ((bf16[64,64,128]{2,1,0:T(8,128)(2,1)}), bf16[64,64,128]{2,1,0:T(8,128)(2,1)S(1)}, u32[]{:S(2)}, u32[]{:S(2)}) async-start(bf16[64,64,128]{2,1,0:T(8,128)(2,1)} %project.1), calls=%async_computation.1 | async-start | bytes 2097152 | tf_op jit(solution)/shard_map/all_to_all | solution.py:24
  75.6 33.9 %copy-start.10 = (f32[72,128]{1,0:T(8,128)S(1)}, f32[72,128]{1,0:T(8,128)}, u32[]{:S(2)}) copy-start(f32[72,128]{1,0:T(8,128)} %constant.57.clone.refs_7_) | copy-start | bytes 110596
  75.6 33.9 %copy-start.11 = (f32[72,128]{1,0:T(8,128)S(1)}, f32[72,128]{1,0:T(8,128)}, u32[]{:S(2)}) copy-start(f32[72,128]{1,0:T(8,128)} %constant.58.clone.refs_8_) | copy-start | bytes 110596
  76.0 33.5 %copy-start.8 = (bf16[64,432]{1,0:T(8,128)(2,1)S(1)}, bf16[64,432]{1,0:T(8,128)(2,1)}, u32[]{:S(2)}) copy-start(bf16[64,432]{1,0:T(8,128)(2,1)} %constant.54.clone.refs_4_) | copy-start | bytes 165892
  76.0 33.5 %copy-start.9 = (bf16[144,128]{1,0:T(8,128)(2,1)S(1)}, bf16[144,128]{1,0:T(8,128)(2,1)}, u32[]{:S(2)}) copy-start(bf16[144,128]{1,0:T(8,128)(2,1)} %constant.53.clone.refs_3_) | copy-start | bytes 110596
  76.0 33.5 %copy-start.6 = (bf16[256,256]{1,0:T(8,128)(2,1)S(1)}, bf16[256,256]{1,0:T(8,128)(2,1)}, u32[]{:S(2)}) copy-start(bf16[256,256]{1,0:T(8,128)(2,1)} %constant.55.clone.refs_5_) | copy-start | bytes 393220
  76.0 33.5 %copy-start.7 = (bf16[256,256]{1,0:T(8,128)(2,1)S(1)}, bf16[256,256]{1,0:T(8,128)(2,1)}, u32[]{:S(2)}) copy-start(bf16[256,256]{1,0:T(8,128)(2,1)} %constant.56.clone.refs_6_) | copy-start | bytes 393220

commit v6 on v5

--- a/solution.py
+++ b/solution.py
@@ -85,13 +85,13 @@
     )
 
 
-def spectrum(rows_ref, items, first, middle_high, middle_low, cos_t, sin_t):
+def spectrum(rows_refs, items, first, middle_high, middle_low, cos_t, sin_t):
     series = jnp.concatenate(
-        [rows_ref[pl.ds(c, HALF, stride=items), :] for c in range(items)], axis=1
+        [ref[pl.ds(c, HALF, stride=items), :] for ref in rows_refs for c in range(items)], axis=1
     ).astype(jnp.bfloat16)
     lines = dot(first, jnp.concatenate([series, series], axis=0))
     turned = []
-    for c in range(items):
+    for c in range(len(rows_refs) * items):
         at = slice(c * INNER, (c + 1) * INNER)
         real, imag = lines[:LINES, at], lines[LINES:, at]
         turned.append(
@@ -130,9 +130,7 @@
     first = first_ref[...]
     cos_t, sin_t = cos_ref[...], sin_ref[...]
     high, low = high_ref[...], low_ref[...]
-    rows_ref[...] = filters
-    filt = spectrum(rows_ref, items, first, high, low, cos_t, sin_t)
-    filt_re, filt_im = filt[:, :inner], filt[:, inner:]
+    back_ref[...] = filters
     values = values.astype(jnp.bfloat16)
     before = dot(values, back_taps_ref[:, :inner], 1, 1)
     filtered = dot(values, back_taps_ref[:, inner:], 1, 1)
@@ -149,7 +147,9 @@
                     at = slice(block * items, (block + 1) * items)
                     piece = (total[i * items : (i + 1) * items] * gates[at]).astype(jnp.bfloat16)
                     rows_ref[at] = piece.astype(jnp.float32)
-    grad = spectrum(rows_ref, items, first, high, low, cos_t, sin_t)
+    both = spectrum((back_ref, rows_ref), items, first, high, low, cos_t, sin_t)
+    filt, grad = both[: items * LINES], both[items * LINES :]
+    filt_re, filt_im = filt[:, :inner], filt[:, inner:]
     grad_re, grad_im = grad[:, :inner], grad[:, inner:]
     both = jnp.concatenate(
         [filt_re * grad_re + filt_im * grad_im, filt_re * grad_im - filt_im * grad_re], axis=1

time: 136 us -> 136 us (level)
  no operation moved by 1% of the time
where the time goes in v6:
time: 136 us
  starting transfers between devices  54 us (40%)
  waiting for transfers between devices  50.2 us (37%)
  blocking collectives  22.1 us (16%)
  Pallas kernels  6.64 us (5%)
  local copies, waits for them, and re-layouts  1.84 us (1%)
    all_to_all x2, waiting for transfers between devices, swap(): return lax.all_to_all(value, axes, split_axis=0, concat_axis=0, tiled=True)  33.8 us
    all_to_all x1, blocking collectives, swap(): return lax.all_to_all(value, axes, split_axis=0, concat_axis=0, tiled=True)  22.1 us
    ppermute x3, starting transfers between devices, flip(): return lax.ppermute(value, axis, [(i, i ^ bit) for i in range(count)])  21.8 us
    all_to_all x2, starting transfers between devices, swap(): return lax.all_to_all(value, axes, split_axis=0, concat_axis=0, tiled=True)  16.6 us
    ppermute x3, starting transfers between devices, local(): blocks.append(lax.ppermute(blocks[0], 'z', ring))  15.6 us
    ppermute x3, waiting for transfers between devices, flip(): return lax.ppermute(value, axis, [(i, i ^ bit) for i in range(count)])  8.7 us
    ppermute x3, waiting for transfers between devices, local(): blocks.append(lax.ppermute(blocks[0], 'z', ring))  7.76 us
    pallas_call x1, Pallas kernels, local(): pl.pallas_call(conv, out_shape=jax.ShapeDtypeStruct((seq_devices, 3 * ite...  3.16 us
  transfers between devices with their start and end apart: 8, of which 5 were waited for; matrix products, arithmetic and copies ran while one was open for 1% of the time, Pallas kernels for 0%

profile of v6, /device:TPU:9, one launch (start us, length us, event | category | flops | bytes accessed | tf_op | source)
XLA Modules:
  0.0 135.8 jit_solution(8804314937101638862)
XLA Ops:
  0.6 0.0 copy-start
  0.7 0.9 copy-done.1
  1.6 0.9 repeat.1
  2.4 7.4 %all-to-all-start = ((bf16[16,128,128]{2,1,0:T(8,128)(2,1)}), bf16[16,128,128]{2,1,0:T(8,128)(2,1)S(1)}, u32[]{:S(2)}, u32[]{:S(2)}) async-start(bf16[16,128,128]{2,1,0:T(8,128)(2,1)} %bitcast.1), calls=%async_computation | async-start | bytes 1048576 | tf_op jit(solution)/shard_map/all_to_all | solution.py:24
  9.8 10.6 %collective-permute-start.1 = (bf16[64,512]{1,0:T(8,128)(2,1)S(1)}, bf16[64,512]{1,0:T(8,128)(2,1)S(1)}, u32[]{:S(2)}, u32[]{:S(2)}) collective-permute-start(bf16[64,512]{1,0:T(8,128)(2,1)S(1)} %bitcast.25), channel_id=1, source_target_pairs={{0,256},{64,320},{128,384},{192,448},{256,0},{320,64},{384,128},{4... | collective-permute-start | bytes 196616 | tf_op jit(solution)/shard_map/ppermute | solution.py:29
  20.4 0.6 all-to-all-done
  21.0 6.3 %collective-permute-start = (bf16[16,128,128]{2,1,0:T(8,128)(2,1)S(1)}, bf16[16,128,128]{2,1,0:T(8,128)(2,1)S(1)}, u32[]{:S(2)}, u32[]{:S(2)}) collective-permute-start(bf16[16,128,128]{2,1,0:T(8,128)(2,1)S(1)} %all-to-all-done), channel_id=1, source_target_pairs={{0,1},{1,0},{2,3},{3,2},{4,5},{5,4},{6,7},{7,6},{8,9},{9,8},{10,11... | collective-permute-start | bytes 1572872 | tf_op jit(solution)/shard_map/ppermute | solution.py:29
  27.4 0.0 copy-start.2
  27.4 0.0 copy-start.3
  27.4 0.0 copy-start.5
  27.4 4.8 %collective-permute-start.2 = (bf16[2,64,512]{2,1,0:T(8,128)(2,1)S(1)}, bf16[2,64,512]{2,1,0:T(8,128)(2,1)S(1)}, u32[]{:S(2)}, u32[]{:S(2)}) collective-permute-start(bf16[2,64,512]{2,1,0:T(8,128)(2,1)S(1)} %pad_maximum_fusion.1), channel_id=1, source_target_pairs={{0,8},{8,0},{1,9},{9,1},{2,10},{10,2},{3,11},{11,3},{4,12},{12,4},... | collective-permute-start | bytes 393224 | tf_op jit(solution)/shard_map/ppermute | solution.py:29
  32.2 8.7 %collective-permute-done.2 = bf16[2,64,512]{2,1,0:T(8,128)(2,1)S(1)} collective-permute-done((bf16[2,64,512]{2,1,0:T(8,128)(2,1)S(1)}, bf16[2,64,512]{2,1,0:T(8,128)(2,1)S(1)}, u32[]{:S(2)}, u32[]{:S(2)}) %collective-permute-start.2) | collective-permute-done | bytes 131104 | tf_op jit(solution)/shard_map/ppermute | solution.py:29
  41.0 5.8 %collective-permute-start.3 = (bf16[4,64,512]{2,1,0:T(8,128)(2,1)S(1)}, bf16[4,64,512]{2,1,0:T(8,128)(2,1)S(1)}, u32[]{:S(2)}, u32[]{:S(2)}) collective-permute-start(bf16[4,64,512]{2,1,0:T(8,128)(2,1)S(1)} %pad_maximum_fusion.rest_0_), channel_id=1, source_target_pairs={{0,128},{64,448},{128,256},{192,64},{256,384},{320,192},{384,0},{4... | collective-permute-start | bytes 786440 | tf_op jit(solution)/shard_map/ppermute | solution.py:263
  46.7 7.0 %collective-permute-start.4 = (bf16[4,64,512]{2,1,0:T(8,128)(2,1)S(1)}, bf16[4,64,512]{2,1,0:T(8,128)(2,1)S(1)}, u32[]{:S(2)}, u32[]{:S(2)}) collective-permute-start(bf16[4,64,512]{2,1,0:T(8,128)(2,1)S(1)} %pad_maximum_fusion.rest_0_), channel_id=1, source_target_pairs={{0,448},{64,0},{128,64},{192,128},{256,192},{320,256},{384,320},{4... | collective-permute-start | bytes 786440 | tf_op jit(solution)/shard_map/ppermute | solution.py:263
  53.8 2.8 %collective-permute-start.5 = (bf16[4,64,512]{2,1,0:T(8,128)(2,1)S(1)}, bf16[4,64,512]{2,1,0:T(8,128)(2,1)S(1)}, u32[]{:S(2)}, u32[]{:S(2)}) collective-permute-start(bf16[4,64,512]{2,1,0:T(8,128)(2,1)S(1)} %pad_maximum_fusion.rest_0_), channel_id=1, source_target_pairs={{0,64},{64,128},{128,192},{192,256},{256,320},{320,384},{384,448},... | collective-permute-start | bytes 786440 | tf_op jit(solution)/shard_map/ppermute | solution.py:263
  56.6 1.2 collective-permute-done.3.rest_1_
  57.8 6.6 %collective-permute-done.4.rest_2_ = bf16[4,64,512]{2,1,0:T(8,128)(2,1)S(1)} collective-permute-done((bf16[4,64,512]{2,1,0:T(8,128)(2,1)S(1)}, bf16[4,64,512]{2,1,0:T(8,128)(2,1)S(1)}, u32[]{:S(2)}, u32[]{:S(2)}) %collective-permute-start.4) | collective-permute-done | bytes 262176 | tf_op jit(solution)/shard_map/ppermute | solution.py:263
  64.4 1.8 %project.1 = bf16[64,64,128]{2,1,0:T(8,128)(2,1)} custom-call(bf16[4,4,128,128]{3,2,1,0:T(8,128)(2,1)S(1)} %bitcast.17, bf16[4,4,128,128]{3,2,1,0:T(8,128)(2,1)S(1)} %bitcast.18, bf16[4,64,512]{2,1,0:T(8,128)(2,1)S(1)} %pad_maximum_fusion.rest_0_, bf16[4,64,512]{2,1,0:T(8,128)(2,1)S(1)} %collective-permute-done.3.rest_1_, ...), custom_call_target="tpu_custom_call" | custom-call | flops 536870912 | bytes 3145728 | tf_op jit(solution)/shard_map/project/pallas_call | solution.py:281
  66.3 9.3 %all-to-all-start.1 = ((bf16[64,64,128]{2,1,0:T(8,128)(2,1)}), bf16[64,64,128]{2,1,0:T(8,128)(2,1)S(1)}, u32[]{:S(2)}, u32[]{:S(2)}) async-start(bf16[64,64,128]{2,1,0:T(8,128)(2,1)} %project.1), calls=%async_computation.1 | async-start | bytes 2097152 | tf_op jit(solution)/shard_map/all_to_all | solution.py:24
  75.6 0.0 copy-start.10
  75.6 0.0 copy-start.11
  75.6 0.3 tile.10
  76.0 0.0 copy-start.8
  76.0 0.0 copy-start.9
  76.0 0.0 copy-start.6
  76.0 0.0 copy-start.7
  76.1 0.2 rev.3.refs_2_
  76.3 33.2 %all-to-all-done.1.refs_0_ = bf16[64,64,128]{2,1,0:T(8,128)(2,1)S(1)} async-done(((bf16[64,64,128]{2,1,0:T(8,128)(2,1)}), bf16[64,64,128]{2,1,0:T(8,128)(2,1)S(1)}, u32[]{:S(2)}, u32[]{:S(2)}) %all-to-all-start.1) | async-done | bytes 1048608 | tf_op jit(solution)/shard_map/all_to_all | solution.py:24
  109.6 3.2 %conv.1 = bf16[64,24,128]{2,1,0:T(8,128)(2,1)S(1)} custom-call(bf16[64,64,128]{2,1,0:T(8,128)(2,1)S(1)} %all-to-all-done.1.refs_0_, bf16[128,256]{1,0:T(8,128)(2,1)S(1)} %reshape.51.refs_1_, bf16[128,256]{1,0:T(8,128)(2,1)S(1)} %rev.3.refs_2_, bf16[144,128]{1,0:T(8,128)(2,1)S(1)} %copy-done.9, bf16[64,432]{1,0:T(8,128)(2,1)S(1)} %copy-done.8, ...), custom_call_target="tpu_custom_call" | custom-call | flops 2147483648 | bytes 4194304 | tf_op jit(solution)/shard_map/conv/pallas_call | solution.py:310
  112.7 0.2 slice.9
  112.9 22.1 %all_to_all.15.home_ref = bf16[64,9,2,128]{3,2,1,0:T(2,128)(2,1)S(1)} all-to-all(bf16[64,9,2,128]{3,2,1,0:T(2,128)(2,1)S(1)} %slice.9), channel_id=1, replica_groups=mesh['z'=8,'x'=4,'yh'=2,'yl'=4,'core'=2] {'z','x','yh'}, dimensions={0} | all-to-all | bytes 589824 | tf_op jit(solution)/shard_map/all_to_all | solution.py:24
  135.1 0.8 unpack.1
  (25 shorter events, 0.1 us)
Async XLA Ops:
  0.6 74.9 %copy-start = (bf16[32,128]{1,0:T(8,128)(2,1)S(1)}, bf16[32,128]{1,0:T(8,128)(2,1)}, u32[]{:S(2)}) copy-start(bf16[32,128]{1,0:T(8,128)(2,1)} %param.19) | copy-start | bytes 24580
  0.6 0.9 copy-start.1
  2.4 7.4 %copy-start.12 = (bf16[512,64]{0,1:T(8,128)(2,1)S(1)}, bf16[512,64]{0,1:T(8,128)(2,1)}, u32[]{:S(2)}) copy-start(bf16[512,64]{0,1:T(8,128)(2,1)} %param.17) | copy-start | bytes 196612
  2.4 18.6 %all-to-all-start = ((bf16[16,128,128]{2,1,0:T(8,128)(2,1)}), bf16[16,128,128]{2,1,0:T(8,128)(2,1)S(1)}, u32[]{:S(2)}, u32[]{:S(2)}) async-start(bf16[16,128,128]{2,1,0:T(8,128)(2,1)} %bitcast.1), calls=%async_computation | async-start | bytes 1048576 | tf_op jit(solution)/shard_map/all_to_all | solution.py:24
  9.8 17.5 %collective-permute-start.1 = (bf16[64,512]{1,0:T(8,128)(2,1)S(1)}, bf16[64,512]{1,0:T(8,128)(2,1)S(1)}, u32[]{:S(2)}, u32[]{:S(2)}) collective-permute-start(bf16[64,512]{1,0:T(8,128)(2,1)S(1)} %bitcast.25), channel_id=1, source_target_pairs={{0,256},{64,320},{128,384},{192,448},{256,0},{320,64},{384,128},{4... | collective-permute-start | bytes 196616 | tf_op jit(solution)/shard_map/ppermute | solution.py:29
  21.0 43.4 %collective-permute-start = (bf16[16,128,128]{2,1,0:T(8,128)(2,1)S(1)}, bf16[16,128,128]{2,1,0:T(8,128)(2,1)S(1)}, u32[]{:S(2)}, u32[]{:S(2)}) collective-permute-start(bf16[16,128,128]{2,1,0:T(8,128)(2,1)S(1)} %all-to-all-done), channel_id=1, source_target_pairs={{0,1},{1,0},{2,3},{3,2},{4,5},{5,4},{6,7},{7,6},{8,9},{9,8},{10,11... | collective-permute-start | bytes 1572872 | tf_op jit(solution)/shard_map/ppermute | solution.py:29
  27.4 37.0 %copy-start.2 = (bf16[512,128]{1,0:T(8,128)(2,1)S(1)}, bf16[512,128]{1,0:T(8,128)(2,1)}, u32[]{:S(2)}) copy-start(bf16[512,128]{1,0:T(8,128)(2,1)} %param.18) | copy-start | bytes 393220
  27.4 37.0 %copy-start.3 = (bf16[512,128]{1,0:T(8,128)(2,1)S(1)}, bf16[512,128]{1,0:T(8,128)(2,1)}, u32[]{:S(2)}) copy-start(bf16[512,128]{1,0:T(8,128)(2,1)} %param.14) | copy-start | bytes 393220
  27.4 37.0 %copy-start.4 = (bf16[512,128]{1,0:T(8,128)(2,1)S(1)}, bf16[512,128]{1,0:T(8,128)(2,1)}, u32[]{:S(2)}) copy-start(bf16[512,128]{1,0:T(8,128)(2,1)} %param.15) | copy-start | bytes 393220
  27.4 37.0 %copy-start.5 = (bf16[512,128]{1,0:T(8,128)(2,1)S(1)}, bf16[512,128]{1,0:T(8,128)(2,1)}, u32[]{:S(2)}) copy-start(bf16[512,128]{1,0:T(8,128)(2,1)} %param.13) | copy-start | bytes 393220
  27.4 13.5 %collective-permute-start.2 = (bf16[2,64,512]{2,1,0:T(8,128)(2,1)S(1)}, bf16[2,64,512]{2,1,0:T(8,128)(2,1)S(1)}, u32[]{:S(2)}, u32[]{:S(2)}) collective-permute-start(bf16[2,64,512]{2,1,0:T(8,128)(2,1)S(1)} %pad_maximum_fusion.1), channel_id=1, source_target_pairs={{0,8},{8,0},{1,9},{9,1},{2,10},{10,2},{3,11},{11,3},{4,12},{12,4},... | collective-permute-start | bytes 393224 | tf_op jit(solution)/shard_map/ppermute | solution.py:29
  41.0 16.8 %collective-permute-start.3 = (bf16[4,64,512]{2,1,0:T(8,128)(2,1)S(1)}, bf16[4,64,512]{2,1,0:T(8,128)(2,1)S(1)}, u32[]{:S(2)}, u32[]{:S(2)}) collective-permute-start(bf16[4,64,512]{2,1,0:T(8,128)(2,1)S(1)} %pad_maximum_fusion.rest_0_), channel_id=1, source_target_pairs={{0,128},{64,448},{128,256},{192,64},{256,384},{320,192},{384,0},{4... | collective-permute-start | bytes 786440 | tf_op jit(solution)/shard_map/ppermute | solution.py:263
  46.7 17.6 %collective-permute-start.4 = (bf16[4,64,512]{2,1,0:T(8,128)(2,1)S(1)}, bf16[4,64,512]{2,1,0:T(8,128)(2,1)S(1)}, u32[]{:S(2)}, u32[]{:S(2)}) collective-permute-start(bf16[4,64,512]{2,1,0:T(8,128)(2,1)S(1)} %pad_maximum_fusion.rest_0_), channel_id=1, source_target_pairs={{0,448},{64,0},{128,64},{192,128},{256,192},{320,256},{384,320},{4... | collective-permute-start | bytes 786440 | tf_op jit(solution)/shard_map/ppermute | solution.py:263
  53.8 10.6 %collective-permute-start.5 = (bf16[4,64,512]{2,1,0:T(8,128)(2,1)S(1)}, bf16[4,64,512]{2,1,0:T(8,128)(2,1)S(1)}, u32[]{:S(2)}, u32[]{:S(2)}) collective-permute-start(bf16[4,64,512]{2,1,0:T(8,128)(2,1)S(1)} %pad_maximum_fusion.rest_0_), channel_id=1, source_target_pairs={{0,64},{64,128},{128,192},{192,256},{256,320},{320,384},{384,448},... | collective-permute-start | bytes 786440 | tf_op jit(solution)/shard_map/ppermute | solution.py:263
  66.3 43.2 %all-to-all-start.1 = ((bf16[64,64,128]{2,1,0:T(8,128)(2,1)}), bf16[64,64,128]{2,1,0:T(8,128)(2,1)S(1)}, u32[]{:S(2)}, u32[]{:S(2)}) async-start(bf16[64,64,128]{2,1,0:T(8,128)(2,1)} %project.1), calls=%async_computation.1 | async-start | bytes 2097152 | tf_op jit(solution)/shard_map/all_to_all | solution.py:24
  75.6 33.9 %copy-start.10 = (f32[72,128]{1,0:T(8,128)S(1)}, f32[72,128]{1,0:T(8,128)}, u32[]{:S(2)}) copy-start(f32[72,128]{1,0:T(8,128)} %constant.57.clone.refs_7_) | copy-start | bytes 110596
  75.6 33.9 %copy-start.11 = (f32[72,128]{1,0:T(8,128)S(1)}, f32[72,128]{1,0:T(8,128)}, u32[]{:S(2)}) copy-start(f32[72,128]{1,0:T(8,128)} %constant.58.clone.refs_8_) | copy-start | bytes 110596
  76.0 33.5 %copy-start.8 = (bf16[64,432]{1,0:T(8,128)(2,1)S(1)}, bf16[64,432]{1,0:T(8,128)(2,1)}, u32[]{:S(2)}) copy-start(bf16[64,432]{1,0:T(8,128)(2,1)} %constant.54.clone.refs_4_) | copy-start | bytes 165892
  76.0 33.5 %copy-start.9 = (bf16[144,128]{1,0:T(8,128)(2,1)S(1)}, bf16[144,128]{1,0:T(8,128)(2,1)}, u32[]{:S(2)}) copy-start(bf16[144,128]{1,0:T(8,128)(2,1)} %constant.53.clone.refs_3_) | copy-start | bytes 110596
  76.0 33.5 %copy-start.6 = (bf16[256,256]{1,0:T(8,128)(2,1)S(1)}, bf16[256,256]{1,0:T(8,128)(2,1)}, u32[]{:S(2)}) copy-start(bf16[256,256]{1,0:T(8,128)(2,1)} %constant.55.clone.refs_5_) | copy-start | bytes 393220
  76.0 33.5 %copy-start.7 = (bf16[256,256]{1,0:T(8,128)(2,1)S(1)}, bf16[256,256]{1,0:T(8,128)(2,1)}, u32[]{:S(2)}) copy-start(bf16[256,256]{1,0:T(8,128)(2,1)} %constant.56.clone.refs_6_) | copy-start | bytes 393220
